TPU v7x, 32 devices: a whole 2x2x4 slice. The times are simulated.
32 devices in a mesh: dp: 8 (over z, x), tensor: 4 (over y, core).
Axes of the slice: x: 2, y: 2, z: 4, core: 2. Of those that a mesh axis runs over, the one named last changes fastest.
Arguments:
- hidden_in: bfloat16 [16384, 768], P(('dp', 'tensor')), may hold values from -6 to 6
- seq_lengths: int32 [32], P('dp'), may hold values from 128 to 512, as said below
- w_query: bfloat16 [768, 768], P('dp', 'tensor'), may hold values from -0.3125 to 0.3125
- b_query: float32 [768], replicated, may hold values from -3 to 3
- w_key: bfloat16 [768, 768], P('dp', 'tensor'), may hold values from -0.3125 to 0.3125
- w_value: bfloat16 [768, 768], P('dp', 'tensor'), may hold values from -0.21875 to 0.21875
- b_value: float32 [768], replicated, may hold values from -2 to 2
- w_out: bfloat16 [768, 768], P('dp', 'tensor'), may hold values from -1.25 to 1.25
- b_out: float32 [768], replicated, may hold values from -2 to 2
- norm1_gain: float32 [768], replicated, may hold values from 0.5 to 1.5
- norm1_bias: float32 [768], replicated, may hold values from -2 to 2
- w_inner: bfloat16 [768, 3072], P('dp', 'tensor'), may hold values from -0.21875 to 0.21875
- b_inner: float32 [3072], replicated, may hold values from -3 to 3
- w_outer: bfloat16 [768, 3072], P('dp', 'tensor'), may hold values from -0.109375 to 0.109375
- b_outer: float32 [768], replicated, may hold values from -2 to 2
- norm2_gain: float32 [768], replicated, may hold values from 0.5 to 1.5
- norm2_bias: float32 [768], replicated, may hold values from -2 to 2
- out_grad: bfloat16 [16384, 768], P(('dp', 'tensor')), may hold values from -6 to 6
Outputs:
- layer_out: bfloat16 [16384, 768], P(('dp', 'tensor'))
- grad_in: float32 [16384, 768], P(('dp', 'tensor'))
- grad_w_query: float32 [768, 768], P('dp', 'tensor')
- grad_b_query: float32 [768], replicated
- grad_w_key: float32 [768, 768], P('dp', 'tensor')
- grad_w_value: float32 [768, 768], P('dp', 'tensor')
- grad_b_value: float32 [768], replicated
- grad_w_out: float32 [768, 768], P('dp', 'tensor')
- grad_b_out: float32 [768], replicated
- grad_norm1_gain: float32 [768], replicated
- grad_norm1_bias: float32 [768], replicated
- grad_w_inner: float32 [768, 3072], P('dp', 'tensor')
- grad_b_inner: float32 [3072], replicated
- grad_w_outer: float32 [768, 3072], P('dp', 'tensor')
- grad_b_outer: float32 [768], replicated
- grad_norm2_gain: float32 [768], replicated
- grad_norm2_bias: float32 [768], replicated
Inputs may be any that keep to these rules, and one draw needn't show every extreme that they name: `seq_lengths`: every sequence has at least 128 valid slots, and one has exactly that many; one sequence is full in every draw.
All inputs are finite; a program needn't handle non-finite values.
Results may differ from a plain program's by a relative error of at most 0.019.
The roundings to bfloat16 on the way count: a program that leaves them out, or rounds other values in their place, can miss the bound.
Values may be sent and summed in bfloat16 or wider, within the bound.
A program may use at most 128 MiB of HBM per device.

v0:
```python
import functools

import jax
import jax.numpy as jnp
from jax import lax
from jax.experimental import pallas as pl
from jax.experimental.pallas import tpu as pltpu
from jax.sharding import PartitionSpec as P

HEAD_DIM = 64


NEG_FILL = -1000000000.0
NORM_EPS = 1e-12


def layer_norm(residual, norm_gain, norm_bias):
    centre = residual - jnp.mean(residual, axis=-1, keepdims=True)
    spread = jnp.mean(centre * centre, axis=-1, keepdims=True)
    return centre * lax.rsqrt(spread + NORM_EPS) * norm_gain + norm_bias


def exact_gelu(values):
    return jax.nn.gelu(values, approximate=False)


def contract_last(first_op, second_op):
    return lax.dot_general(
        first_op, second_op, (((1,), (1,)), ((), ())), preferred_element_type=jnp.float32
    )


def contract_first(first_op, second_op):
    return lax.dot_general(
        first_op, second_op, (((0,), (0,)), ((), ())), preferred_element_type=jnp.float32
    )


def split_blocks(heads_arr, block_rows):
    batches, length, head_size = heads_arr.shape
    return heads_arr.reshape(batches, length // block_rows, block_rows, head_size).transpose(
        1, 0, 2, 3
    )


def join_blocks(block_array):
    block_count, batches, block_rows, head_size = block_array.shape
    return block_array.transpose(1, 0, 2, 3).reshape(batches, block_count * block_rows, head_size)


def block_scores(query_portion, key_head_tensor, key_valid, score_scale):
    scores = (
        jnp.einsum(
            "eix,evx->eiv", query_portion, key_head_tensor, preferred_element_type=jnp.float32
        )
        * score_scale
    )
    return jnp.where(key_valid[:, None, :], scores, NEG_FILL)


def attend(query_heads, key_head_tensor, value_head_tensor, key_valid, block_rows, score_scale):

    def one_block(query_portion):
        scores = block_scores(query_portion, key_head_tensor, key_valid, score_scale)
        row_max = jnp.max(scores, axis=-1, keepdims=True)
        exponent = jnp.exp(scores - row_max)
        row_total = jnp.sum(exponent, axis=-1, keepdims=True)
        softmax_reduced = (exponent / row_total).astype(jnp.bfloat16)
        mixture = jnp.einsum(
            "fwj,fjt->fwt", softmax_reduced, value_head_tensor, preferred_element_type=jnp.float32
        )
        return (mixture.astype(jnp.bfloat16), row_max, row_total)

    mixture, row_max, row_total = lax.map(one_block, split_blocks(query_heads, block_rows))
    return (join_blocks(mixture), row_max, row_total)


def attend_back(
    query_heads,
    key_head_tensor,
    value_head_tensor,
    grad_heads,
    row_max,
    row_total,
    key_valid,
    block_rows,
    score_scale,
):

    def one_block(running, block_in):
        key_grad, value_grad = running
        query_portion, gradient_portion, max_part, total_part = block_in
        scores = block_scores(query_portion, key_head_tensor, key_valid, score_scale)
        softmax = jnp.exp(scores - max_part) / total_part
        softmax_reduced = softmax.astype(jnp.bfloat16)
        soft_grad = jnp.einsum(
            "eix,evx->eiv", gradient_portion, value_head_tensor, preferred_element_type=jnp.float32
        )
        centre = jnp.sum(softmax * soft_grad, axis=-1, keepdims=True)
        score_gradient = (softmax * (soft_grad - centre)).astype(jnp.bfloat16)
        query_grad = (
            jnp.einsum(
                "fwj,fjt->fwt", score_gradient, key_head_tensor, preferred_element_type=jnp.float32
            )
            * score_scale
        )
        key_grad = (
            key_grad
            + jnp.einsum(
                "oxl,oxn->oln", score_gradient, query_portion, preferred_element_type=jnp.float32
            )
            * score_scale
        )
        value_grad = value_grad + jnp.einsum(
            "oxl,oxn->oln", softmax_reduced, gradient_portion, preferred_element_type=jnp.float32
        )
        return ((key_grad, value_grad), query_grad)

    zero_grads = jnp.zeros(key_head_tensor.shape, jnp.float32)
    block_inputs = (
        split_blocks(query_heads, block_rows),
        split_blocks(grad_heads, block_rows),
        row_max,
        row_total,
    )
    (key_grad, value_grad), query_grad = lax.scan(one_block, (zero_grads, zero_grads), block_inputs)
    return (join_blocks(query_grad), key_grad, value_grad)


def per_device(
    hidden_in,
    seq_lengths,
    w_query,
    b_query,
    w_key,
    w_value,
    b_value,
    w_out,
    b_out,
    norm1_gain,
    norm1_bias,
    w_inner,
    b_inner,
    w_outer,
    b_outer,
    norm2_gain,
    norm2_bias,
    out_grad,
):
    tensor_size = lax.axis_size("tensor")
    tensor_place = lax.axis_index("tensor")
    local_rows, feature_width = hidden_in.shape
    group_rows = local_rows * tensor_size
    seq_count = seq_lengths.shape[0]
    seq_len = group_rows // seq_count
    head_cols = w_query.shape[1]
    inner_cols = w_inner.shape[1]
    heads_here = head_cols // HEAD_DIM
    block_rows = min(512, seq_len)
    score_scale = HEAD_DIM ** (-0.5)
    local_start = tensor_place * local_rows
    row_index = lax.iota(jnp.int32, group_rows)
    seq_match = (row_index[:, None] // seq_len == lax.iota(jnp.int32, seq_count)[None, :]).astype(
        jnp.int32
    )
    row_limit = jnp.sum(seq_match * seq_lengths[None, :], axis=1)
    row_valid = row_index % seq_len < row_limit
    local_mask = lax.dynamic_slice_in_dim(row_valid, local_start, local_rows).astype(jnp.float32)[
        :, None
    ]
    key_valid = jnp.repeat(row_valid.reshape(seq_count, seq_len), heads_here, axis=0)

    def heads_of(matrix):
        shaped = matrix.reshape(seq_count, seq_len, heads_here, HEAD_DIM).transpose(0, 2, 1, 3)
        return shaped.reshape(seq_count * heads_here, seq_len, HEAD_DIM)

    def rows_of(matrix):
        shaped = matrix.reshape(seq_count, heads_here, seq_len, HEAD_DIM).transpose(0, 2, 1, 3)
        return shaped.reshape(group_rows, head_cols)

    full_query, full_key, full_value, full_out, full_inner, full_outer = (
        lax.all_gather(w_query, "dp", axis=0, tiled=True),
        lax.all_gather(w_key, "dp", axis=0, tiled=True),
        lax.all_gather(w_value, "dp", axis=0, tiled=True),
        lax.all_gather(w_out, "dp", axis=0, tiled=True),
        lax.all_gather(w_inner, "dp", axis=0, tiled=True),
        lax.all_gather(w_outer, "dp", axis=0, tiled=True),
    )
    joint_weight = jnp.concatenate((full_query, full_key, full_value), axis=1)
    query_bias = lax.dynamic_slice_in_dim(b_query, tensor_place * head_cols, head_cols)
    value_bias = lax.dynamic_slice_in_dim(b_value, tensor_place * head_cols, head_cols)
    inner_bias = lax.dynamic_slice_in_dim(b_inner, tensor_place * inner_cols, inner_cols)
    joint_bias = jnp.concatenate((query_bias, jnp.zeros((head_cols,), jnp.float32), value_bias))
    whole_in = lax.all_gather(hidden_in, "tensor", axis=0, tiled=True)
    joint_rows = (
        jnp.dot(whole_in, joint_weight, preferred_element_type=jnp.float32) + joint_bias
    ).astype(jnp.bfloat16)
    query_heads = heads_of(joint_rows[:, :head_cols])
    key_head_tensor = heads_of(joint_rows[:, head_cols : 2 * head_cols])
    value_head_tensor = heads_of(joint_rows[:, 2 * head_cols :])
    mixture_heads, row_max, row_total = attend(
        query_heads, key_head_tensor, value_head_tensor, key_valid, block_rows, score_scale
    )
    mixture = rows_of(mixture_heads)
    summed_out = lax.psum_scatter(
        contract_last(mixture, full_out).astype(jnp.bfloat16),
        "tensor",
        scatter_dimension=0,
        tiled=True,
    ).astype(jnp.float32)
    first_sum = hidden_in.astype(jnp.float32) + (summed_out + b_out)
    first_norm = layer_norm(first_sum, norm1_gain, norm1_bias)
    mid_whole = lax.all_gather(first_norm.astype(jnp.bfloat16), "tensor", axis=0, tiled=True)
    pre_act = jnp.dot(mid_whole, full_inner, preferred_element_type=jnp.float32) + inner_bias
    act_low = exact_gelu(pre_act).astype(jnp.bfloat16)
    second_sum = first_norm + (
        lax.psum_scatter(
            contract_last(act_low, full_outer).astype(jnp.bfloat16),
            "tensor",
            scatter_dimension=0,
            tiled=True,
        ).astype(jnp.float32)
        + b_outer
    )
    normed, norm2_back = jax.vjp(layer_norm, second_sum, norm2_gain, norm2_bias)
    layer_out = (normed * local_mask).astype(jnp.bfloat16)
    out_cot = out_grad.astype(jnp.float32) * local_mask
    dsecond, gain2_part, bias2_part = norm2_back(out_cot)
    dffn_low = dsecond.astype(jnp.bfloat16)
    outer_bias_part = jnp.sum(dffn_low, axis=0, dtype=jnp.float32)
    dffn_whole = lax.all_gather(dffn_low, "tensor", axis=0, tiled=True)
    grad_outer = contract_first(dffn_whole, act_low)
    dact = jnp.dot(dffn_whole, full_outer, preferred_element_type=jnp.float32)
    _, gelu_back = jax.vjp(exact_gelu, pre_act)
    dpre_low = gelu_back(dact)[0].astype(jnp.bfloat16)
    inner_bias_part = jnp.sum(dpre_low, axis=0, dtype=jnp.float32)
    grad_inner = contract_first(mid_whole, dpre_low)
    dfirst_norm = dsecond + lax.psum_scatter(
        contract_last(dpre_low, full_inner).astype(jnp.bfloat16),
        "tensor",
        scatter_dimension=0,
        tiled=True,
    ).astype(jnp.float32)
    _, norm1_back = jax.vjp(layer_norm, first_sum, norm1_gain, norm1_bias)
    dfirst, gain1_part, bias1_part = norm1_back(dfirst_norm)
    dattn_low = dfirst.astype(jnp.bfloat16)
    out_bias_part = jnp.sum(dattn_low, axis=0, dtype=jnp.float32)
    dattn_whole = lax.all_gather(dattn_low, "tensor", axis=0, tiled=True)
    grad_out_w = contract_first(dattn_whole, mixture)
    dmixture = jnp.dot(dattn_whole, full_out, preferred_element_type=jnp.float32).astype(
        jnp.bfloat16
    )
    dquery_heads, dkey_heads, dvalue_heads = attend_back(
        query_heads,
        key_head_tensor,
        value_head_tensor,
        heads_of(dmixture),
        row_max,
        row_total,
        key_valid,
        block_rows,
        score_scale,
    )
    djoint = jnp.concatenate(
        (rows_of(dquery_heads), rows_of(dkey_heads), rows_of(dvalue_heads)), axis=1
    ).astype(jnp.bfloat16)
    joint_bias_part = jnp.sum(djoint, axis=0, dtype=jnp.float32)
    grad_joint = contract_first(whole_in, djoint)
    grad_in = dfirst + lax.psum_scatter(
        contract_last(djoint, joint_weight).astype(jnp.bfloat16),
        "tensor",
        scatter_dimension=0,
        tiled=True,
    ).astype(jnp.float32)
    grad_query = grad_joint[:, :head_cols]
    grad_key = grad_joint[:, head_cols : 2 * head_cols]
    grad_value = grad_joint[:, 2 * head_cols :]
    shard_grads = tuple(
        (
            lax.psum_scatter(grad_query, "dp", scatter_dimension=0, tiled=True),
            lax.psum_scatter(grad_key, "dp", scatter_dimension=0, tiled=True),
            lax.psum_scatter(grad_value, "dp", scatter_dimension=0, tiled=True),
            lax.psum_scatter(grad_out_w, "dp", scatter_dimension=0, tiled=True),
            lax.psum_scatter(grad_inner, "dp", scatter_dimension=0, tiled=True),
            lax.psum_scatter(grad_outer, "dp", scatter_dimension=0, tiled=True),
        )
    )

    def placed(vector, total_len):
        return lax.dynamic_update_slice_in_dim(
            jnp.zeros((total_len,), jnp.float32), vector, tensor_place * vector.shape[0], 0
        )

    query_bias_part = placed(joint_bias_part[:head_cols], feature_width)
    value_bias_part = placed(joint_bias_part[2 * head_cols :], feature_width)
    hidden_bias_part = placed(inner_bias_part, b_inner.shape[0])
    vector_sums = lax.psum(
        (
            query_bias_part,
            value_bias_part,
            out_bias_part,
            gain1_part,
            bias1_part,
            hidden_bias_part,
            outer_bias_part,
            gain2_part,
            bias2_part,
        ),
        ("dp", "tensor"),
    )
    return (
        layer_out,
        grad_in,
        shard_grads[0],
        vector_sums[0],
        shard_grads[1],
        shard_grads[2],
        vector_sums[1],
        shard_grads[3],
        vector_sums[2],
        vector_sums[3],
        vector_sums[4],
        shard_grads[4],
        vector_sums[5],
        shard_grads[5],
        vector_sums[6],
        vector_sums[7],
        vector_sums[8],
    )


Z_SIZE = 4
MESH_IDS = pl.DeviceIdType.MESH


def flip(place, bit):
    return place + bit - 2 * place * bit


class Place:
    def __init__(self):
        self.dp = lax.axis_index("dp")
        self.t = lax.axis_index("tensor")
        self.z = self.dp // 2
        self.x = self.dp % 2
        self.y = self.t // 2
        self.c = self.t % 2

    def chip(self, dz, da, db):
        c = self.c
        z = lax.rem(self.z - dz + Z_SIZE, Z_SIZE)
        x = flip(self.x, da * c + db * (1 - c))
        y = flip(self.y, da * (1 - c) + db * c)
        return z * 2 + x, y

    def device(self, dz=0, da=0, db=0, other=False):
        dp, y = self.chip(dz, da, db)
        core = 1 - self.c if other else self.c
        return {"dp": dp, "tensor": y * 2 + core}


def block_of(ref, m, dp, t, rows):
    return ref.at[m, t, pl.ds(pl.multiple_of(dp * rows, rows), rows), :]


def meet(me):
    barrier = pltpu.get_barrier_semaphore()
    peers = [me.device(dz=k) for k in range(1, Z_SIZE)]
    peers += [me.device(da=1), me.device(db=1), me.device(other=True)]
    for peer in peers:
        pl.semaphore_signal(barrier, inc=1, device_id=peer, device_id_type=MESH_IDS)
    pl.semaphore_wait(barrier, len(peers))


def remote(src, dst, send, recv, peer):
    return pltpu.make_async_remote_copy(
        src_ref=src, dst_ref=dst, send_sem=send, recv_sem=recv, device_id=peer, device_id_type=MESH_IDS
    )


def gather_kernel(p_ref, i_ref, o_ref, g_ref, send_sem, recv_sem, local_sem):
    me = Place()
    rows = p_ref.shape[0]
    c = me.c
    shards = (p_ref, i_ref, o_ref)

    def send(m, slot, src, chip, core, peer):
        dst = block_of(g_ref, m, chip[0], chip[1] * 2 + core, rows)
        remote(src, dst, send_sem.at[m, slot], recv_sem.at[m, slot], peer).start()

    def own(m, slot, peer):
        send(m, slot, shards[m], me.chip(0, 0, 0), c, peer)

    def forward(m, slot, dz, da, db, peer):
        chip = me.chip(dz, da, db)
        send(m, slot, block_of(g_ref, m, chip[0], chip[1] * 2 + c, rows), chip, c, peer)

    def arrived(m, slot):
        any_block = block_of(g_ref, m, 0, 0, rows)
        remote(any_block, any_block, send_sem.at[m, slot], recv_sem.at[m, slot], me.device(db=1)).wait_recv()

    def left(m, slot):
        any_block = block_of(g_ref, m, 0, 0, rows)
        remote(any_block, any_block, send_sem.at[m, slot], recv_sem.at[m, slot], me.device(db=1)).wait_send()

    meet(me)
    copies = []
    for m in range(3):
        for k in range(1, Z_SIZE):
            own(m, k, me.device(dz=Z_SIZE - k))
        own(m, 4, me.device(da=1))
        own(m, 8, me.device(db=1))
        own(m, 16, me.device(other=True))
        copy = pltpu.make_async_copy(shards[m], block_of(g_ref, m, me.dp, me.t, rows), local_sem.at[m])
        copy.start()
        copies.append(copy)
    for m in range(3):

        @pl.loop(1, Z_SIZE)
        def _(k):
            arrived(m, k)
            forward(m, 4 + k, k, 0, 0, me.device(da=1))
            forward(m, 8 + 2 * k, k, 0, 0, me.device(db=1))
            forward(m, 16 + 4 * k, k, 0, 0, me.device(other=True))

        @pl.loop(0, Z_SIZE)
        def _(k):
            arrived(m, 4 + k)
            forward(m, 9 + 2 * k, k, 1, 0, me.device(db=1))
            forward(m, 18 + 4 * k, k, 1, 0, me.device(other=True))

        @pl.loop(0, 2 * Z_SIZE)
        def _(s):
            arrived(m, 8 + s)
            forward(m, 17 + 2 * s, s // 2, s % 2, 1, me.device(other=True))

    for m in range(3):
        copies[m].wait()

        @pl.loop(16, 32)
        def _(s):
            arrived(m, s)

        @pl.loop(1, 32)
        def _(s):
            left(m, s)


def gather_all(packed, inner, outer, n_dp, n_t):
    rows, width = packed.shape
    return pl.pallas_call(
        gather_kernel,
        out_shape=jax.ShapeDtypeStruct((3, n_t, n_dp * rows, width), jnp.bfloat16),
        in_specs=[pl.BlockSpec(memory_space=pltpu.VMEM)] * 3,
        out_specs=pl.BlockSpec(memory_space=pltpu.VMEM),
        scratch_shapes=[
            pltpu.SemaphoreType.DMA((3, 32)),
            pltpu.SemaphoreType.DMA((3, 32)),
            pltpu.SemaphoreType.DMA((3,)),
        ],
        compiler_params=pltpu.CompilerParams(
            collective_id=0, has_side_effects=True, vmem_limit_bytes=60 * 2**20
        ),
    )(packed, inner, outer)


def scatter_kernel(g_ref, v_ref, out_ref, vout_ref, core_buf, b_buf, a_buf, z_buf, vec_buf, vec_z, send_sem, recv_sem, vec_send, vec_recv):
    me = Place()
    n_m, rows = out_ref.shape[0], out_ref.shape[1]
    c = me.c

    def part(m, dz, da, db, core):
        dp, y = me.chip(dz, da, db)
        return block_of(g_ref, m, dp, y * 2 + core, rows)

    def wait(m, slot):
        one = z_buf.at[m, 1]
        return remote(one, one, send_sem.at[m, slot], recv_sem.at[m, slot], me.device(db=1))

    def go(m, slot, src, dst, peer):
        remote(src, dst, send_sem.at[m, slot], recv_sem.at[m, slot], peer).start()

    def vec(step, src, dst, peer):
        return remote(src, dst, vec_send.at[step], vec_recv.at[step], peer)

    meet(me)
    partner = me.device(other=True)
    for m in range(n_m):
        for pick in (1, 0):

            @pl.loop(0, 8)
            def _(s):
                slot = 2 * s + pick
                go(m, slot, part(m, s // 2, s % 2, pick, 1 - c), core_buf.at[m, slot], partner)

    def from_core(m, dz, da, db):
        return 4 * dz + 2 * db + da

    for m in range(n_m):

        @pl.loop(0, 8)
        def _(s):
            dz, da = s // 2, s % 2
            slot = from_core(m, dz, da, 1)
            wait(m, slot).wait_recv()
            core_buf[m, slot] = part(m, dz, da, 1, c)[...] + core_buf[m, slot]
            go(m, 16 + s, core_buf.at[m, slot], b_buf.at[m, s], me.device(db=1))

        @pl.loop(0, 8)
        def _(s):
            dz, da = s // 2, s % 2
            slot = from_core(m, dz, da, 0)
            wait(m, slot).wait_recv()
            core_buf[m, slot] = part(m, dz, da, 0, c)[...] + core_buf[m, slot]

        @pl.loop(0, Z_SIZE)
        def _(k):
            wait(m, 16 + 2 * k + 1).wait_recv()
            b_buf[m, 2 * k + 1] = b_buf[m, 2 * k + 1] + core_buf[m, from_core(m, k, 1, 0)]
            go(m, 24 + k, b_buf.at[m, 2 * k + 1], a_buf.at[m, k], me.device(da=1))

        @pl.loop(0, Z_SIZE)
        def _(k):
            wait(m, 16 + 2 * k).wait_recv()
            b_buf[m, 2 * k] = b_buf[m, 2 * k] + core_buf[m, from_core(m, k, 0, 0)]

        @pl.loop(1, Z_SIZE)
        def _(k):
            wait(m, 24 + k).wait_recv()
            a_buf[m, k] = a_buf[m, k] + b_buf[m, 2 * k]
            go(m, 28 + k, a_buf.at[m, k], z_buf.at[m, k], me.device(dz=k))

        wait(m, 24).wait_recv()
        a_buf[m, 0] = a_buf[m, 0] + b_buf[m, 0]

    def peer_of(dx, dy):
        return {"dp": me.z * 2 + flip(me.x, dx), "tensor": 2 * flip(me.y, dy) + c}

    vec_buf[0] = v_ref[...]
    for step, peer in enumerate((partner, peer_of(1, 0), peer_of(0, 1))):
        copy = vec(step, vec_buf.at[2 * step], vec_buf.at[2 * step + 1], peer)
        copy.start()
        copy.wait()
        vec_buf[2 * step + 2] = vec_buf[2 * step] + vec_buf[2 * step + 1]
    vec_z[me.z] = vec_buf[6]
    zcopies = [vec(2 + k, vec_buf.at[6], vec_z.at[me.z], me.device(dz=k)) for k in range(1, Z_SIZE)]
    for copy in zcopies:
        copy.start()
    for copy in zcopies:
        copy.wait()
    vout_ref[...] = (vec_z[0] + vec_z[1]) + (vec_z[2] + vec_z[3])

    for m in range(n_m):
        total = a_buf[m, 0].astype(jnp.float32)
        for k in range(1, Z_SIZE):
            wait(m, 28 + k).wait_recv()
            total = total + z_buf[m, k].astype(jnp.float32)
        out_ref[m] = total

        @pl.loop(0, 28)
        def _(s):
            wait(m, s).wait_send()

        @pl.loop(29, 32)
        def _(s):
            wait(m, s).wait_send()


def scatter_all(grads, vector, n_dp):
    n_m, n_t, total_rows, width = grads.shape
    rows = total_rows // n_dp
    buf = lambda n: pltpu.VMEM((n_m, n, rows, width), jnp.bfloat16)
    return pl.pallas_call(
        scatter_kernel,
        out_shape=(
            jax.ShapeDtypeStruct((n_m, rows, width), jnp.float32),
            jax.ShapeDtypeStruct(vector.shape, jnp.float32),
        ),
        in_specs=[pl.BlockSpec(memory_space=pltpu.VMEM)] * 2,
        out_specs=[pl.BlockSpec(memory_space=pltpu.VMEM)] * 2,
        scratch_shapes=[
            buf(16),
            buf(8),
            buf(4),
            buf(4),
            pltpu.VMEM((7,) + vector.shape, jnp.float32),
            pltpu.VMEM((Z_SIZE,) + vector.shape, jnp.float32),
            pltpu.SemaphoreType.DMA((n_m, 32)),
            pltpu.SemaphoreType.DMA((n_m, 32)),
            pltpu.SemaphoreType.DMA((6,)),
            pltpu.SemaphoreType.DMA((6,)),
        ],
        compiler_params=pltpu.CompilerParams(
            collective_id=1, has_side_effects=True, vmem_limit_bytes=60 * 2**20
        ),
    )(grads, vector)


def dot_nn(a, b):
    return lax.dot_general(a, b, (((1,), (0,)), ((), ())), preferred_element_type=jnp.float32)


def dot_nt(a, b):
    return lax.dot_general(a, b, (((1,), (1,)), ((), ())), preferred_element_type=jnp.float32)


def dot_tn(a, b):
    return lax.dot_general(a, b, (((0,), (0,)), ((), ())), preferred_element_type=jnp.float32)


def low(a):
    return a.astype(jnp.bfloat16)


def row_mean(a):
    return jnp.mean(a, axis=-1, keepdims=True)


def normalise(r):
    centre = r - row_mean(r)
    inverse = lax.rsqrt(row_mean(centre * centre) + NORM_EPS)
    return centre * inverse, inverse


def norm_back(g, z, inverse):
    return (g - row_mean(g) - z * row_mean(g * z)) * inverse


def gelu_pair(u):
    cdf = 0.5 + 0.5 * lax.erf(u * (0.5**0.5))
    density = jnp.exp(-0.5 * u * u) * ((0.5 / jnp.pi) ** 0.5)
    return u * cdf, cdf + u * density


V_BQ, V_BV, V_BO, V_G1, V_B1, V_BF, V_G2, V_B2, V_BI = range(9)
TILE = 64


class Layer:
    def __init__(self, **refs):
        self.__dict__.update(refs)
        self.rows, self.width = self.x.shape
        self.n_t = self.w.shape[1]
        self.cols = self.width // self.n_t
        self.heads = self.cols // HEAD_DIM
        self.ocol = (3 * self.cols) // 128 * 128

    def tiles(self, body):
        @pl.loop(0, self.rows // TILE)
        def _(i):
            body(pl.ds(pl.multiple_of(i * TILE, TILE), TILE))

    def project(self, t):
        lane = lax.broadcasted_iota(jnp.int32, (1, self.width), 1)
        out = dot_nn(self.x[...], self.w[0, t]) + self.qkv_bias[t]
        self.qkv[t] = low(jnp.where(lane < 3 * self.cols, out, 0.0))

    def piece(self, t, which, j):
        first = which * self.cols + j * HEAD_DIM
        return self.qkv.at[t, :, first : first + HEAD_DIM]

    def attend(self, t, valid):
        self.att[t, :, : HEAD_DIM] = jnp.zeros((self.rows, HEAD_DIM), jnp.bfloat16)
        for j in range(self.heads):
            q, k, v = (self.piece(t, i, j)[...] for i in range(3))
            s = dot_nt(k, q * jnp.bfloat16(HEAD_DIM**-0.5))
            s = jnp.where(valid, s, NEG_FILL)
            e = jnp.exp(s - jnp.max(s, axis=0, keepdims=True))
            p = low(e * (1.0 / jnp.sum(e, axis=0, keepdims=True)))
            self.p[t * self.heads + j] = p
            mix = dot_tn(v, p)
            first = 3 * self.cols - self.ocol + j * HEAD_DIM
            self.att[t, :, first : first + HEAD_DIM] = low(mix.T)

    def out_project(self, t):
        self.acc[...] += dot_nt(self.att[t], self.w[0, t, :, self.ocol :])

    def start_residual(self):
        self.acc[...] = self.x[...].astype(jnp.float32) + self.vec[2:3, :]

    def first_norm(self):
        def body(r):
            z, inverse = normalise(self.acc[r, :])
            self.z1[r, :] = z
            self.inv1[r, :] = jnp.broadcast_to(inverse, (TILE, 128))
            h1 = z * self.vec[3:4, :] + self.vec[4:5, :]
            self.h1b[r, :] = low(h1)
            self.acc[r, :] = h1 + self.vec[0:1, :]

        self.tiles(body)

    def inner(self, t):
        @pl.loop(0, self.rows // 128)
        def _(i):
            r = pl.ds(pl.multiple_of(i * 128, 128), 128)
            pre = dot_nn(self.h1b[r, :], self.w[1, t]) + self.inner_bias[t]
            act, slope = gelu_pair(pre)
            self.act[t, r, :] = low(act)
            self.slope[t, r, :] = low(slope)

    def outer(self, t):
        self.acc[...] += dot_nt(self.act[t], self.w[2, t])

    def second_norm(self, length):
        self.sums[...] = jnp.zeros_like(self.sums)

        def body(r):
            z, inverse = normalise(self.acc[r, :])
            place = r.start + lax.broadcasted_iota(jnp.int32, (TILE, 1), 0)
            mask = (place < length).astype(jnp.float32)
            gain = self.vec[5:6, :]
            self.y[r, :] = low((z * gain + self.vec[6:7, :]) * mask)
            dy = self.og[r, :].astype(jnp.float32) * mask
            dr2 = norm_back(dy * gain, z, inverse)
            self.acc[r, :] = dr2
            df = low(dr2)
            self.df[r, :] = df
            self.sums[V_G2] += fold(dy * z)
            self.sums[V_B2] += fold(dy)
            self.sums[V_BF] += fold(df.astype(jnp.float32))

        self.tiles(body)

    def outer_back(self, t):
        self.dact[...] = dot_nn(self.df[...], self.w[2, t])

        def body(r):
            d = low(self.dact[r, :] * self.slope[t, r, :].astype(jnp.float32))
            self.slope[t, r, :] = d
            self.sums[V_BI + t] += fold(d.astype(jnp.float32))

        self.tiles(body)
        self.w[2, t] = low(dot_nn(self.df_t[...], self.act[t]))

    def inner_back(self, t):
        self.acc[...] += dot_nt(self.slope[t], self.w[1, t])
        self.w[1, t] = low(dot_nn(self.h1b_t[...], self.slope[t]))

    def first_norm_back(self):
        def body(r):
            z = self.z1[r, :]
            dh1 = self.acc[r, :]
            self.sums[V_G1] += fold(dh1 * z)
            self.sums[V_B1] += fold(dh1)
            dr1 = norm_back(dh1 * self.vec[3:4, :], z, self.inv1[r, :1])
            self.acc[r, :] = dr1
            dob = low(dr1)
            self.df[r, :] = dob
            self.sums[V_BO] += fold(dob.astype(jnp.float32))

        self.tiles(body)

    def attend_back(self, t):
        scale = HEAD_DIM**-0.5
        self.datt[...] = low(dot_nn(self.df[...], self.w[0, t, :, self.ocol :]))
        for j in range(self.heads):
            first = 3 * self.cols - self.ocol + j * HEAD_DIM
            d = self.datt[:, first : first + HEAD_DIM]
            q, k, v = (self.piece(t, i, j)[...] for i in range(3))
            p = self.p[t * self.heads + j]
            dp = dot_nt(v, d)
            pf = p.astype(jnp.float32)
            delta = jnp.sum(pf * dp, axis=0, keepdims=True)
            ds = low(pf * (dp - delta))
            self.piece(t, 2, j)[...] = low(dot_nn(p, d))
            self.piece(t, 1, j)[...] = low(dot_nn(ds, q) * scale)
            self.piece(t, 0, j)[...] = low((dot_tn(k, ds) * scale).T)

    def project_back(self, t):
        self.acc[...] += dot_nt(self.qkv[t], self.w[0, t])

        def body(r):
            self.sums[V_BI + self.n_t + t] += fold(self.qkv[t, r, :].astype(jnp.float32))

        self.tiles(body)
        self.w[0, t] = low(dot_nn(self.x_t[...], self.qkv[t]))
        out = self.w.at[0, t, :, self.ocol :]
        out[...] = low(out[...].astype(jnp.float32) + dot_nn(self.df_t[...], self.att[t]))

    def transpose(self, src, dst):
        dst[...] = src[...].T


def fold(a):
    return jnp.sum(a.reshape(a.shape[0] // 8, 8, a.shape[1]), axis=0)


def layer_kernel(
    length_ref, x_ref, og_ref, w_in, qkv_bias, inner_bias, vec_ref,
    y_ref, acc_ref, w_ref, sums_ref,
    qkv, p, att, z1, inv1, h1b, act, slope, df, datt, dact, x_t, h1b_t, df_t, sems,
):
    copies = [pltpu.make_async_copy(w_in.at[m], w_ref.at[m], sems.at[m]) for m in range(3)]
    for copy in copies:
        copy.start()
    a = Layer(
        x=x_ref, og=og_ref, w=w_ref, qkv_bias=qkv_bias, inner_bias=inner_bias, vec=vec_ref, y=y_ref, acc=acc_ref, sums=sums_ref,
        qkv=qkv, p=p, att=att, z1=z1, inv1=inv1, h1b=h1b, act=act, slope=slope, df=df, datt=datt, dact=dact, x_t=x_t, h1b_t=h1b_t, df_t=df_t,
    )
    length = length_ref[0]
    valid = lax.broadcasted_iota(jnp.int32, (a.rows, 1), 0) < length
    loop = pl.loop(0, a.n_t)
    a.transpose(a.x, a.x_t)
    a.start_residual()
    copies[0].wait()

    @loop
    def _(t):
        a.project(t)
        a.attend(t, valid)
        a.out_project(t)

    a.first_norm()
    a.transpose(a.h1b, a.h1b_t)
    copies[1].wait()
    copies[2].wait()

    @loop
    def _(t):
        a.inner(t)
        a.outer(t)

    a.second_norm(length)
    a.transpose(a.df, a.df_t)

    @loop
    def _(t):
        a.outer_back(t)
        a.inner_back(t)

    a.first_norm_back()
    a.transpose(a.df, a.df_t)

    @loop
    def _(t):
        a.attend_back(t)
        a.project_back(t)


def layer(length, x, og, whole, qkv_bias, inner_bias, vec):
    rows, width = x.shape
    n_t = whole.shape[1]
    cols = width // n_t
    heads = width // HEAD_DIM
    owidth = width - (3 * cols) // 128 * 128
    bf, f32 = jnp.bfloat16, jnp.float32
    vmem = pl.BlockSpec(memory_space=pltpu.VMEM)
    return pl.pallas_call(
        layer_kernel,
        out_shape=(
            jax.ShapeDtypeStruct((rows, width), bf),
            jax.ShapeDtypeStruct((rows, width), f32),
            jax.ShapeDtypeStruct(whole.shape, bf),
            jax.ShapeDtypeStruct((V_BI + 2 * n_t, 8, width), f32),
        ),
        in_specs=[pl.BlockSpec(memory_space=pltpu.SMEM), vmem, vmem, pl.BlockSpec(memory_space=pl.ANY), vmem, vmem, vmem],
        out_specs=[vmem] * 4,
        scratch_shapes=[
            pltpu.VMEM((n_t, rows, width), bf),
            pltpu.VMEM((heads, rows, rows), bf),
            pltpu.VMEM((n_t, rows, owidth), bf),
            pltpu.VMEM((rows, width), f32),
            pltpu.VMEM((rows, 128), f32),
            pltpu.VMEM((rows, width), bf),
            pltpu.VMEM((n_t, rows, width), bf),
            pltpu.VMEM((n_t, rows, width), bf),
            pltpu.VMEM((rows, width), bf),
            pltpu.VMEM((rows, owidth), bf),
            pltpu.VMEM((rows, width), f32),
            pltpu.VMEM((width, rows), bf),
            pltpu.VMEM((width, rows), bf),
            pltpu.VMEM((width, rows), bf),
            pltpu.SemaphoreType.DMA((3,)),
        ],
        compiler_params=pltpu.CompilerParams(vmem_limit_bytes=63 * 2**20),
    )(length, x, og, whole, qkv_bias, inner_bias, vec)


def data_parallel(
    hidden_in, seq_lengths, w_query, b_query, w_key, w_value, b_value, w_out, b_out, norm1_gain, norm1_bias,
    w_inner, b_inner, w_outer, b_outer, norm2_gain, norm2_bias, out_grad,
):
    n_dp, n_t = lax.axis_size("dp"), lax.axis_size("tensor")
    rows, width = hidden_in.shape
    cols = w_query.shape[1]
    length = lax.dynamic_slice_in_dim(seq_lengths, lax.axis_index("tensor"), 1)
    packed = jnp.concatenate((w_query, w_key, w_value, w_out), axis=1)
    whole = gather_all(packed, w_inner, w_outer, n_dp, n_t)
    split = lambda a: a.reshape(n_t, 1, -1)
    zeros = jnp.zeros((n_t, 1, cols), jnp.float32)
    qkv_bias = jnp.concatenate((split(b_query), zeros, split(b_value), zeros), axis=2)
    vec = jnp.stack((b_outer, b_outer, b_out, norm1_gain, norm1_bias, norm2_gain, norm2_bias, b_out))
    y, grad_in, grads, sums = layer(length, hidden_in, out_grad, whole, qkv_bias, split(b_inner), vec)
    shards, sums = scatter_all(grads, sums.sum(axis=1), n_dp)
    heads = sums[V_BI + n_t :]
    join = lambda a: a.reshape(-1)
    gq, gk, gv, go = (shards[0, :, i * cols : (i + 1) * cols] for i in range(4))
    return (
        y, grad_in, gq, join(heads[:, :cols]), gk, gv, join(heads[:, 2 * cols : 3 * cols]), go, sums[V_BO], sums[V_G1], sums[V_B1],
        shards[1], join(sums[V_BI : V_BI + n_t]), shards[2], sums[V_BF], sums[V_G2], sums[V_B2],
    )


def solution(mesh):
    in_specs = (
        P(("dp", "tensor"), None),
        P("dp"),
        P("dp", "tensor"),
        P(),
        P("dp", "tensor"),
        P("dp", "tensor"),
        P(),
        P("dp", "tensor"),
        P(),
        P(),
        P(),
        P("dp", "tensor"),
        P(),
        P("dp", "tensor"),
        P(),
        P(),
        P(),
        P(("dp", "tensor"), None),
    )
    out_specs = (
        P(("dp", "tensor"), None),
        P(("dp", "tensor"), None),
        P("dp", "tensor"),
        P(),
        P("dp", "tensor"),
        P("dp", "tensor"),
        P(),
        P("dp", "tensor"),
        P(),
        P(),
        P(),
        P("dp", "tensor"),
        P(),
        P("dp", "tensor"),
        P(),
        P(),
        P(),
    )
    small = mesh.shape["dp"] == 2 * Z_SIZE and mesh.shape["tensor"] == 4
    return jax.shard_map(
        data_parallel if small else per_device, mesh=mesh, in_specs=in_specs, out_specs=out_specs, check_vma=False
    )
```

profile of v0, /device:TPU:0, one launch (start us, length us, event | category | flops | bytes accessed | tf_op | source)
XLA Modules:
  0.0 280.1 jit_solution(1496435873063050084)
XLA Ops:
  0.7 1.2 dynamic_slice.3.length_ref
  1.9 0.7 stack.24
  2.6 0.7 stack.25
  3.3 0.7 stack.26
  4.0 0.7 stack.23
  4.7 0.7 stack.27
  5.3 0.7 stack.28
  6.0 0.8 reshape.52
  6.8 0.8 reshape.53
  7.6 0.7 pad_maximum_fusion.1.qkv_bias
  8.3 0.6 stack.29.vec_ref
  8.9 1.6 pad_maximum_fusion.p_ref
  10.5 76.9 %shard_map.305.w_in = bf16[3,4,768,768]{3,2,1,0:T(8,128)(2,1)} custom-call(bf16[96,768]{1,0:T(8,128)(2,1)} %pad_maximum_fusion.p_ref, bf16[96,768]{1,0:T(8,128)(2,1)} %i_ref.1, bf16[96,768]{1,0:T(8,128)(2,1)} %o_ref.1), custom_call_target="tpu_custom_call" | custom-call | tf_op jit(solution)/shard_map/pallas_call | solution.py:451
  87.4 73.5 %shard_map.306 = (bf16[512,768]{1,0:T(8,128)(2,1)}, f32[512,768]{1,0:T(8,128)}, bf16[3,4,768,768]{3,2,1,0:T(8,128)(2,1)}, f32[16,8,768]{2,1,0:T(8,128)}) custom-call(s32[1]{0:T(128)} %dynamic_slice.3.length_ref, bf16[512,768]{1,0:T(8,128)(2,1)} %x_ref.1, bf16[512,768]{1,0:T(8,128)(2,1)} %og_ref.1, bf16[3,4,768,768]{3,2,1,0:T(8,128)(2,1)} %shard_map.305.w_in, ...), custom_call_target="tpu_custom_call" | custom-call | tf_op jit(solution)/shard_map/pallas_call | solution.py:848
  160.9 1.7 reduce_sum.9.v_ref
  162.6 108.7 %shard_map.307 = (f32[3,96,768]{2,1,0:T(8,128)}, f32[16,768]{1,0:T(8,128)}) custom-call(bf16[3,4,768,768]{3,2,1,0:T(8,128)(2,1)} %get-tuple-element.25.g_ref, f32[16,768]{1,0:T(8,128)} %reduce_sum.9.v_ref), custom_call_target="tpu_custom_call" | custom-call | tf_op jit(solution)/shard_map/pallas_call | solution.py:573
  271.4 0.7 fusion
  272.1 0.7 reshape.56
  272.7 0.7 reshape.55
  273.4 0.7 slice.58
  274.2 1.6 slice_reduce_fusion
  275.8 0.6 reshape.57
  276.4 1.9 slice_bitcast_fusion.2
  278.2 1.9 slice_bitcast_fusion
  (1 shorter events, 0.0 us)
where the time goes:
time: 281 us; the launch traced here: 280 us
  Pallas kernels  259 us (92%)
  local copies, waits for them, and re-layouts  16.3 us (6%)
  other arithmetic  4.04 us (1%)
    pallas_call x1, Pallas kernels, scatter_all(): pl.pallas_call(scatter_kernel, out_shape=(jax.ShapeDtypeStruct((n_m, rows...  109 us
    pallas_call x1, Pallas kernels, gather_all(): pl.pallas_call(gather_kernel, out_shape=jax.ShapeDtypeStruct((3, n_t, n_d...  76.9 us
    pallas_call x1, Pallas kernels, layer(): pl.pallas_call(layer_kernel, out_shape=(jax.ShapeDtypeStruct((rows, width...  73.5 us

commit v1 on v0

--- a/solution.py
+++ b/solution.py
@@ -378,222 +378,221 @@
     )
 
 
-def gather_kernel(p_ref, i_ref, o_ref, g_ref, send_sem, recv_sem, local_sem):
-    me = Place()
-    rows = p_ref.shape[0]
-    c = me.c
-    shards = (p_ref, i_ref, o_ref)
-
-    def send(m, slot, src, chip, core, peer):
-        dst = block_of(g_ref, m, chip[0], chip[1] * 2 + core, rows)
-        remote(src, dst, send_sem.at[m, slot], recv_sem.at[m, slot], peer).start()
-
-    def own(m, slot, peer):
-        send(m, slot, shards[m], me.chip(0, 0, 0), c, peer)
-
-    def forward(m, slot, dz, da, db, peer):
-        chip = me.chip(dz, da, db)
-        send(m, slot, block_of(g_ref, m, chip[0], chip[1] * 2 + c, rows), chip, c, peer)
-
-    def arrived(m, slot):
-        any_block = block_of(g_ref, m, 0, 0, rows)
-        remote(any_block, any_block, send_sem.at[m, slot], recv_sem.at[m, slot], me.device(db=1)).wait_recv()
-
-    def left(m, slot):
-        any_block = block_of(g_ref, m, 0, 0, rows)
-        remote(any_block, any_block, send_sem.at[m, slot], recv_sem.at[m, slot], me.device(db=1)).wait_send()
-
-    meet(me)
-    copies = []
-    for m in range(3):
-        for k in range(1, Z_SIZE):
-            own(m, k, me.device(dz=Z_SIZE - k))
-        own(m, 4, me.device(da=1))
-        own(m, 8, me.device(db=1))
-        own(m, 16, me.device(other=True))
-        copy = pltpu.make_async_copy(shards[m], block_of(g_ref, m, me.dp, me.t, rows), local_sem.at[m])
-        copy.start()
-        copies.append(copy)
-    for m in range(3):
-
-        @pl.loop(1, Z_SIZE)
-        def _(k):
-            arrived(m, k)
-            forward(m, 4 + k, k, 0, 0, me.device(da=1))
-            forward(m, 8 + 2 * k, k, 0, 0, me.device(db=1))
-            forward(m, 16 + 4 * k, k, 0, 0, me.device(other=True))
-
+class Gather:
+    def __init__(self, me, shards, w, send_sem, recv_sem, local_sem):
+        self.me, self.shards, self.w = me, shards, w
+        self.send_sem, self.recv_sem, self.local_sem = send_sem, recv_sem, local_sem
+        self.rows = shards[0].shape[0]
+
+    def block(self, m, chip, core):
+        return block_of(self.w, m, chip[0], chip[1] * 2 + core, self.rows)
+
+    def send(self, m, slot, src, chip, peer):
+        dst = self.block(m, chip, self.me.c)
+        remote(src, dst, self.send_sem.at[m, slot], self.recv_sem.at[m, slot], peer).start()
+
+    def own(self, m, slot, peer):
+        self.send(m, slot, self.shards[m], self.me.chip(0, 0, 0), peer)
+
+    def forward(self, m, slot, dz, da, db, peer):
+        chip = self.me.chip(dz, da, db)
+        self.send(m, slot, self.block(m, chip, self.me.c), chip, peer)
+
+    def slot(self, m, slot):
+        one = block_of(self.w, m, 0, 0, self.rows)
+        return remote(one, one, self.send_sem.at[m, slot], self.recv_sem.at[m, slot], self.me.device(db=1))
+
+    def local(self, m):
+        me = self.me
+        dst = block_of(self.w, m, me.dp, me.t, self.rows)
+        return pltpu.make_async_copy(self.shards[m], dst, self.local_sem.at[m])
+
+    def begin(self):
+        me = self.me
+        for m in range(3):
+            for k in range(1, Z_SIZE):
+                self.own(m, k, me.device(dz=Z_SIZE - k))
+            self.own(m, 4, me.device(da=1))
+            self.own(m, 8, me.device(db=1))
+            self.own(m, 16, me.device(other=True))
+            self.local(m).start()
+
+    def pump(self, m, s):
+        me = self.me
+        self.slot(m, s).wait_recv()
+
+        @pl.when(s < 4)
+        def _():
+            self.forward(m, 4 + s, s, 0, 0, me.device(da=1))
+            self.forward(m, 8 + 2 * s, s, 0, 0, me.device(db=1))
+            self.forward(m, 16 + 4 * s, s, 0, 0, me.device(other=True))
+
+        @pl.when((s >= 4) & (s < 8))
+        def _():
+            k = s - 4
+            self.forward(m, 9 + 2 * k, k, 1, 0, me.device(db=1))
+            self.forward(m, 18 + 4 * k, k, 1, 0, me.device(other=True))
+
+        @pl.when(s >= 8)
+        def _():
+            k = s - 8
+            self.forward(m, 17 + 2 * k, k // 2, k % 2, 1, me.device(other=True))
+
+    def pumps(self, m, first, last):
+        @pl.loop(first, last)
+        def _(s):
+            self.pump(m, s)
+
+    def collect(self, m):
+        self.local(m).wait()
+
+        @pl.loop(16, 32)
+        def _(s):
+            self.slot(m, s).wait_recv()
+
+    def drain(self):
+        for m in range(3):
+
+            @pl.loop(1, 32)
+            def _(s):
+                self.slot(m, s).wait_send()
+
+
+class Scatter:
+    def __init__(self, me, w, core_buf, b_buf, a_buf, z_buf, send_sem, recv_sem):
+        self.me, self.w = me, w
+        self.core_buf, self.b_buf, self.a_buf, self.z_buf = core_buf, b_buf, a_buf, z_buf
+        self.send_sem, self.recv_sem = send_sem, recv_sem
+        self.rows = z_buf.shape[2]
+
+    def order(self, i):
+        me = self.me
+        mine = i // 2
+        core = flip(1 - me.c, mine)
+        return flip(me.y, 1 - i % 2) * 2 + core
+
+    def part(self, m, dz, da, db, core):
+        dp, y = self.me.chip(dz, da, db)
+        return block_of(self.w, m, dp, y * 2 + core, self.rows)
+
+    def wait(self, m, slot):
+        one = self.z_buf.at[m, 1]
+        return remote(one, one, self.send_sem.at[m, slot], self.recv_sem.at[m, slot], self.me.device(db=1))
+
+    def go(self, m, slot, src, dst, peer):
+        remote(src, dst, self.send_sem.at[m, slot], self.recv_sem.at[m, slot], peer).start()
+
+    def from_core(self, dz, da, db):
+        return 4 * dz + 2 * db + da
+
+    def ready(self, m, i):
+        me = self.me
+        c = me.c
+        side = 1 - i % 2
+
+        @pl.when(i < 2)
+        def _():
+            @pl.loop(0, 8)
+            def _(s):
+                dz, other = s // 2, s % 2
+                da = side * (1 - c) + other * c
+                db = other * (1 - c) + side * c
+                slot = 4 * dz + 2 * da + db
+                self.go(m, slot, self.part(m, dz, da, db, 1 - c), self.core_buf.at[m, slot], me.device(other=True))
+
+        @pl.when(i >= 2)
+        def _():
+            @pl.loop(0, 8)
+            def _(s):
+                dz, other = s // 2, s % 2
+                da = side * (1 - c) + other * c
+                db = other * (1 - c) + side * c
+                slot = self.from_core(dz, da, db)
+                self.wait(m, slot).wait_recv()
+                self.core_buf[m, slot] = self.part(m, dz, da, db, c)[...] + self.core_buf[m, slot]
+
+                @pl.when(db == 1)
+                def _():
+                    place = 2 * dz + da
+                    self.go(m, 16 + place, self.core_buf.at[m, slot], self.b_buf.at[m, place], me.device(db=1))
+
+    def b_step(self, m, k):
+        for da in (1, 0):
+            self.wait(m, 16 + 2 * k + da).wait_recv()
+            self.b_buf[m, 2 * k + da] = self.b_buf[m, 2 * k + da] + self.core_buf[m, self.from_core(k, da, 0)]
+            if da:
+                self.go(m, 24 + k, self.b_buf.at[m, 2 * k + 1], self.a_buf.at[m, k], self.me.device(da=1))
+
+    def a_step(self, m, k):
+        self.wait(m, 24 + k).wait_recv()
+        self.a_buf[m, k] = self.a_buf[m, k] + self.b_buf[m, 2 * k]
+
+        @pl.when(k > 0)
+        def _():
+            self.go(m, 28 + k, self.a_buf.at[m, k], self.z_buf.at[m, k], self.me.device(dz=k))
+
+    def steps(self, step, m):
         @pl.loop(0, Z_SIZE)
         def _(k):
-            arrived(m, 4 + k)
-            forward(m, 9 + 2 * k, k, 1, 0, me.device(db=1))
-            forward(m, 18 + 4 * k, k, 1, 0, me.device(other=True))
-
-        @pl.loop(0, 2 * Z_SIZE)
-        def _(s):
-            arrived(m, 8 + s)
-            forward(m, 17 + 2 * s, s // 2, s % 2, 1, me.device(other=True))
-
-    for m in range(3):
-        copies[m].wait()
-
-        @pl.loop(16, 32)
-        def _(s):
-            arrived(m, s)
-
-        @pl.loop(1, 32)
-        def _(s):
-            left(m, s)
-
-
-def gather_all(packed, inner, outer, n_dp, n_t):
-    rows, width = packed.shape
-    return pl.pallas_call(
-        gather_kernel,
-        out_shape=jax.ShapeDtypeStruct((3, n_t, n_dp * rows, width), jnp.bfloat16),
-        in_specs=[pl.BlockSpec(memory_space=pltpu.VMEM)] * 3,
-        out_specs=pl.BlockSpec(memory_space=pltpu.VMEM),
-        scratch_shapes=[
-            pltpu.SemaphoreType.DMA((3, 32)),
-            pltpu.SemaphoreType.DMA((3, 32)),
-            pltpu.SemaphoreType.DMA((3,)),
-        ],
-        compiler_params=pltpu.CompilerParams(
-            collective_id=0, has_side_effects=True, vmem_limit_bytes=60 * 2**20
-        ),
-    )(packed, inner, outer)
-
-
-def scatter_kernel(g_ref, v_ref, out_ref, vout_ref, core_buf, b_buf, a_buf, z_buf, vec_buf, vec_z, send_sem, recv_sem, vec_send, vec_recv):
-    me = Place()
-    n_m, rows = out_ref.shape[0], out_ref.shape[1]
-    c = me.c
-
-    def part(m, dz, da, db, core):
-        dp, y = me.chip(dz, da, db)
-        return block_of(g_ref, m, dp, y * 2 + core, rows)
-
-    def wait(m, slot):
-        one = z_buf.at[m, 1]
-        return remote(one, one, send_sem.at[m, slot], recv_sem.at[m, slot], me.device(db=1))
-
-    def go(m, slot, src, dst, peer):
-        remote(src, dst, send_sem.at[m, slot], recv_sem.at[m, slot], peer).start()
-
-    def vec(step, src, dst, peer):
-        return remote(src, dst, vec_send.at[step], vec_recv.at[step], peer)
-
-    meet(me)
-    partner = me.device(other=True)
-    for m in range(n_m):
-        for pick in (1, 0):
-
-            @pl.loop(0, 8)
+            step(m, k)
+
+    def finish(self, m, out_ref):
+        total = self.a_buf[m, 0].astype(jnp.float32)
+        for k in range(1, Z_SIZE):
+            self.wait(m, 28 + k).wait_recv()
+            total = total + self.z_buf[m, k].astype(jnp.float32)
+        out_ref[m] = total
+
+    def drain(self):
+        for m in range(3):
+
+            @pl.loop(0, 28)
             def _(s):
-                slot = 2 * s + pick
-                go(m, slot, part(m, s // 2, s % 2, pick, 1 - c), core_buf.at[m, slot], partner)
-
-    def from_core(m, dz, da, db):
-        return 4 * dz + 2 * db + da
-
-    for m in range(n_m):
-
-        @pl.loop(0, 8)
-        def _(s):
-            dz, da = s // 2, s % 2
-            slot = from_core(m, dz, da, 1)
-            wait(m, slot).wait_recv()
-            core_buf[m, slot] = part(m, dz, da, 1, c)[...] + core_buf[m, slot]
-            go(m, 16 + s, core_buf.at[m, slot], b_buf.at[m, s], me.device(db=1))
-
-        @pl.loop(0, 8)
-        def _(s):
-            dz, da = s // 2, s % 2
-            slot = from_core(m, dz, da, 0)
-            wait(m, slot).wait_recv()
-            core_buf[m, slot] = part(m, dz, da, 0, c)[...] + core_buf[m, slot]
-
-        @pl.loop(0, Z_SIZE)
-        def _(k):
-            wait(m, 16 + 2 * k + 1).wait_recv()
-            b_buf[m, 2 * k + 1] = b_buf[m, 2 * k + 1] + core_buf[m, from_core(m, k, 1, 0)]
-            go(m, 24 + k, b_buf.at[m, 2 * k + 1], a_buf.at[m, k], me.device(da=1))
-
-        @pl.loop(0, Z_SIZE)
-        def _(k):
-            wait(m, 16 + 2 * k).wait_recv()
-            b_buf[m, 2 * k] = b_buf[m, 2 * k] + core_buf[m, from_core(m, k, 0, 0)]
-
-        @pl.loop(1, Z_SIZE)
-        def _(k):
-            wait(m, 24 + k).wait_recv()
-            a_buf[m, k] = a_buf[m, k] + b_buf[m, 2 * k]
-            go(m, 28 + k, a_buf.at[m, k], z_buf.at[m, k], me.device(dz=k))
-
-        wait(m, 24).wait_recv()
-        a_buf[m, 0] = a_buf[m, 0] + b_buf[m, 0]
-
-    def peer_of(dx, dy):
-        return {"dp": me.z * 2 + flip(me.x, dx), "tensor": 2 * flip(me.y, dy) + c}
-
-    vec_buf[0] = v_ref[...]
-    for step, peer in enumerate((partner, peer_of(1, 0), peer_of(0, 1))):
-        copy = vec(step, vec_buf.at[2 * step], vec_buf.at[2 * step + 1], peer)
-        copy.start()
-        copy.wait()
-        vec_buf[2 * step + 2] = vec_buf[2 * step] + vec_buf[2 * step + 1]
-    vec_z[me.z] = vec_buf[6]
-    zcopies = [vec(2 + k, vec_buf.at[6], vec_z.at[me.z], me.device(dz=k)) for k in range(1, Z_SIZE)]
-    for copy in zcopies:
-        copy.start()
-    for copy in zcopies:
-        copy.wait()
-    vout_ref[...] = (vec_z[0] + vec_z[1]) + (vec_z[2] + vec_z[3])
-
-    for m in range(n_m):
-        total = a_buf[m, 0].astype(jnp.float32)
+                self.wait(m, s).wait_send()
+
+            @pl.loop(29, 32)
+            def _(s):
+                self.wait(m, s).wait_send()
+
+
+class VectorSum:
+    def __init__(self, me, buf, zbuf, send_sem, recv_sem):
+        self.me, self.buf, self.zbuf, self.send_sem, self.recv_sem = me, buf, zbuf, send_sem, recv_sem
+
+    def copy(self, step, src, dst, peer):
+        return remote(src, dst, self.send_sem.at[step], self.recv_sem.at[step], peer)
+
+    def peer(self, step):
+        me = self.me
+        if step == 0:
+            return me.device(other=True)
+        dx, dy = ((1, 0), (0, 1))[step - 1]
+        return {"dp": me.z * 2 + flip(me.x, dx), "tensor": 2 * flip(me.y, dy) + me.c}
+
+    def pair(self, step):
+        return self.copy(step, self.buf.at[2 * step], self.buf.at[2 * step + 1], self.peer(step))
+
+    def start(self, value):
+        self.buf[0] = value
+        self.pair(0).start()
+
+    def advance(self, step):
+        self.pair(step).wait()
+        self.buf[2 * step + 2] = self.buf[2 * step] + self.buf[2 * step + 1]
+        if step < 2:
+            self.pair(step + 1).start()
+        else:
+            self.zbuf[self.me.z] = self.buf[6]
+            for k in range(1, Z_SIZE):
+                self.z_copy(k).start()
+
+    def z_copy(self, k):
+        return self.copy(2 + k, self.buf.at[6], self.zbuf.at[self.me.z], self.me.device(dz=k))
+
+    def result(self):
         for k in range(1, Z_SIZE):
-            wait(m, 28 + k).wait_recv()
-            total = total + z_buf[m, k].astype(jnp.float32)
-        out_ref[m] = total
-
-        @pl.loop(0, 28)
-        def _(s):
-            wait(m, s).wait_send()
-
-        @pl.loop(29, 32)
-        def _(s):
-            wait(m, s).wait_send()
-
-
-def scatter_all(grads, vector, n_dp):
-    n_m, n_t, total_rows, width = grads.shape
-    rows = total_rows // n_dp
-    buf = lambda n: pltpu.VMEM((n_m, n, rows, width), jnp.bfloat16)
-    return pl.pallas_call(
-        scatter_kernel,
-        out_shape=(
-            jax.ShapeDtypeStruct((n_m, rows, width), jnp.float32),
-            jax.ShapeDtypeStruct(vector.shape, jnp.float32),
-        ),
-        in_specs=[pl.BlockSpec(memory_space=pltpu.VMEM)] * 2,
-        out_specs=[pl.BlockSpec(memory_space=pltpu.VMEM)] * 2,
-        scratch_shapes=[
-            buf(16),
-            buf(8),
-            buf(4),
-            buf(4),
-            pltpu.VMEM((7,) + vector.shape, jnp.float32),
-            pltpu.VMEM((Z_SIZE,) + vector.shape, jnp.float32),
-            pltpu.SemaphoreType.DMA((n_m, 32)),
-            pltpu.SemaphoreType.DMA((n_m, 32)),
-            pltpu.SemaphoreType.DMA((6,)),
-            pltpu.SemaphoreType.DMA((6,)),
-        ],
-        compiler_params=pltpu.CompilerParams(
-            collective_id=1, has_side_effects=True, vmem_limit_bytes=60 * 2**20
-        ),
-    )(grads, vector)
+            self.z_copy(k).wait()
+        return (self.zbuf[0] + self.zbuf[1]) + (self.zbuf[2] + self.zbuf[3])
 
 
 def dot_nn(a, b):
@@ -659,7 +658,7 @@
         first = which * self.cols + j * HEAD_DIM
         return self.qkv.at[t, :, first : first + HEAD_DIM]
 
-    def attend(self, t, valid):
+    def attend(self, t, valid, between):
         self.att[t, :, : HEAD_DIM] = jnp.zeros((self.rows, HEAD_DIM), jnp.bfloat16)
         for j in range(self.heads):
             q, k, v = (self.piece(t, i, j)[...] for i in range(3))
@@ -671,6 +670,7 @@
             mix = dot_tn(v, p)
             first = 3 * self.cols - self.ocol + j * HEAD_DIM
             self.att[t, :, first : first + HEAD_DIM] = low(mix.T)
+            between(j)
 
     def out_project(self, t):
         self.acc[...] += dot_nt(self.att[t], self.w[0, t, :, self.ocol :])
@@ -750,7 +750,7 @@
 
         self.tiles(body)
 
-    def attend_back(self, t):
+    def attend_back(self, t, between):
         scale = HEAD_DIM**-0.5
         self.datt[...] = low(dot_nn(self.df[...], self.w[0, t, :, self.ocol :]))
         for j in range(self.heads):
@@ -765,6 +765,7 @@
             self.piece(t, 2, j)[...] = low(dot_nn(p, d))
             self.piece(t, 1, j)[...] = low(dot_nn(ds, q) * scale)
             self.piece(t, 0, j)[...] = low((dot_tn(k, ds) * scale).T)
+            between(j)
 
     def project_back(self, t):
         self.acc[...] += dot_nt(self.qkv[t], self.w[0, t])
@@ -785,77 +786,131 @@
     return jnp.sum(a.reshape(a.shape[0] // 8, 8, a.shape[1]), axis=0)
 
 
-def layer_kernel(
-    length_ref, x_ref, og_ref, w_in, qkv_bias, inner_bias, vec_ref,
-    y_ref, acc_ref, w_ref, sums_ref,
-    qkv, p, att, z1, inv1, h1b, act, slope, df, datt, dact, x_t, h1b_t, df_t, sems,
+def step_kernel(
+    length_ref, x_ref, og_ref, packed_ref, wi_ref, wo_ref, qkv_bias, inner_bias, vec_ref,
+    y_ref, acc_ref, out_ref, vout_ref,
+    w, sums, qkv, p, att, z1, inv1, h1b, act, slope, df, datt, dact, x_t, h1b_t, df_t,
+    core_buf, b_buf, a_buf, z_buf, vec_buf, vec_z,
+    gather_send, gather_recv, local_sem, send_sem, recv_sem, vec_send, vec_recv,
 ):
-    copies = [pltpu.make_async_copy(w_in.at[m], w_ref.at[m], sems.at[m]) for m in range(3)]
-    for copy in copies:
-        copy.start()
+    me = Place()
+    gather = Gather(me, (packed_ref, wi_ref, wo_ref), w, gather_send, gather_recv, local_sem)
+    scatter = Scatter(me, w, core_buf, b_buf, a_buf, z_buf, send_sem, recv_sem)
+    small = VectorSum(me, vec_buf, vec_z, vec_send, vec_recv)
+    meet(me)
+    gather.begin()
     a = Layer(
-        x=x_ref, og=og_ref, w=w_ref, qkv_bias=qkv_bias, inner_bias=inner_bias, vec=vec_ref, y=y_ref, acc=acc_ref, sums=sums_ref,
+        x=x_ref, og=og_ref, w=w, qkv_bias=qkv_bias, inner_bias=inner_bias, vec=vec_ref, y=y_ref, acc=acc_ref, sums=sums,
         qkv=qkv, p=p, att=att, z1=z1, inv1=inv1, h1b=h1b, act=act, slope=slope, df=df, datt=datt, dact=dact, x_t=x_t, h1b_t=h1b_t, df_t=df_t,
     )
     length = length_ref[0]
     valid = lax.broadcasted_iota(jnp.int32, (a.rows, 1), 0) < length
-    loop = pl.loop(0, a.n_t)
     a.transpose(a.x, a.x_t)
     a.start_residual()
-    copies[0].wait()
-
-    @loop
+    gather.pumps(0, 1, 16)
+    gather.collect(0)
+
+    @pl.loop(0, a.n_t)
     def _(t):
         a.project(t)
-        a.attend(t, valid)
+        a.attend(t, valid, lambda j: gather.pump(1, a.heads * t + j + 1))
         a.out_project(t)
 
+    gather.pumps(1, 1 + a.n_t * a.heads, 16)
     a.first_norm()
     a.transpose(a.h1b, a.h1b_t)
-    copies[1].wait()
-    copies[2].wait()
-
-    @loop
+    gather.pumps(2, 1, 4)
+    gather.collect(1)
+
+    @pl.loop(0, a.n_t)
     def _(t):
+        gather.pumps(2, 4 + 3 * t, 7 + 3 * t)
         a.inner(t)
+
+    gather.collect(2)
+
+    @pl.loop(0, a.n_t)
+    def _(t):
         a.outer(t)
 
     a.second_norm(length)
     a.transpose(a.df, a.df_t)
-
-    @loop
-    def _(t):
-        a.outer_back(t)
-        a.inner_back(t)
+    gather.drain()
+
+    @pl.loop(0, a.n_t)
+    def _(i):
+        a.outer_back(scatter.order(i))
+        scatter.ready(2, i)
+
+    @pl.loop(0, a.n_t)
+    def _(i):
+        a.inner_back(scatter.order(i))
+        scatter.ready(1, i)
 
     a.first_norm_back()
     a.transpose(a.df, a.df_t)
 
-    @loop
-    def _(t):
-        a.attend_back(t)
+    def between(i, j):
+        n = a.heads * i + j
+
+        @pl.when(n < 4)
+        def _():
+            scatter.b_step(2, n)
+
+        @pl.when((n >= 4) & (n < 8))
+        def _():
+            scatter.a_step(2, n - 4)
+
+        @pl.when((n >= 6) & (n < 10))
+        def _():
+            scatter.b_step(1, n - 6)
+
+    @pl.loop(0, a.n_t)
+    def _(i):
+        t = scatter.order(i)
+        a.attend_back(t, lambda j: between(i, j))
         a.project_back(t)
-
-
-def layer(length, x, og, whole, qkv_bias, inner_bias, vec):
+        scatter.ready(0, i)
+
+    small.start(jnp.sum(sums[...], axis=1))
+    scatter.steps(scatter.a_step, 1)
+    small.advance(0)
+    scatter.steps(scatter.b_step, 0)
+    small.advance(1)
+    scatter.steps(scatter.a_step, 0)
+    small.advance(2)
+    for m in (2, 1):
+        scatter.finish(m, out_ref)
+    vout_ref[...] = small.result()
+    scatter.finish(0, out_ref)
+    scatter.drain()
+
+
+def step(length, x, og, packed, inner, outer, qkv_bias, inner_bias, vec, n_t):
     rows, width = x.shape
-    n_t = whole.shape[1]
     cols = width // n_t
     heads = width // HEAD_DIM
     owidth = width - (3 * cols) // 128 * 128
+    shard = packed.shape[0]
     bf, f32 = jnp.bfloat16, jnp.float32
     vmem = pl.BlockSpec(memory_space=pltpu.VMEM)
+    n_v = V_BI + 2 * n_t
+    n_w = shard * lax.axis_size("dp")
+    buf = lambda n: pltpu.VMEM((3, n, shard, width), bf)
+    dma = pltpu.SemaphoreType.DMA
     return pl.pallas_call(
-        layer_kernel,
+        step_kernel,
         out_shape=(
             jax.ShapeDtypeStruct((rows, width), bf),
             jax.ShapeDtypeStruct((rows, width), f32),
-            jax.ShapeDtypeStruct(whole.shape, bf),
-            jax.ShapeDtypeStruct((V_BI + 2 * n_t, 8, width), f32),
+            jax.ShapeDtypeStruct((3, shard, width), f32),
+            jax.ShapeDtypeStruct((n_v, width), f32),
         ),
-        in_specs=[pl.BlockSpec(memory_space=pltpu.SMEM), vmem, vmem, pl.BlockSpec(memory_space=pl.ANY), vmem, vmem, vmem],
+        in_specs=[pl.BlockSpec(memory_space=pltpu.SMEM)] + [vmem] * 8,
         out_specs=[vmem] * 4,
         scratch_shapes=[
+            pltpu.VMEM((3, n_t, n_w, width), bf),
+            pltpu.VMEM((n_v, 8, width), f32),
             pltpu.VMEM((n_t, rows, width), bf),
             pltpu.VMEM((heads, rows, rows), bf),
             pltpu.VMEM((n_t, rows, owidth), bf),
@@ -870,28 +925,39 @@
             pltpu.VMEM((width, rows), bf),
             pltpu.VMEM((width, rows), bf),
             pltpu.VMEM((width, rows), bf),
-            pltpu.SemaphoreType.DMA((3,)),
+            buf(16),
+            buf(8),
+            buf(4),
+            buf(4),
+            pltpu.VMEM((7, n_v, width), f32),
+            pltpu.VMEM((Z_SIZE, n_v, width), f32),
+            dma((3, 32)),
+            dma((3, 32)),
+            dma((3,)),
+            dma((3, 32)),
+            dma((3, 32)),
+            dma((6,)),
+            dma((6,)),
         ],
-        compiler_params=pltpu.CompilerParams(vmem_limit_bytes=63 * 2**20),
-    )(length, x, og, whole, qkv_bias, inner_bias, vec)
+        compiler_params=pltpu.CompilerParams(collective_id=0, has_side_effects=True, vmem_limit_bytes=63 * 2**20),
+    )(length, x, og, packed, inner, outer, qkv_bias, inner_bias, vec)
 
 
 def data_parallel(
     hidden_in, seq_lengths, w_query, b_query, w_key, w_value, b_value, w_out, b_out, norm1_gain, norm1_bias,
     w_inner, b_inner, w_outer, b_outer, norm2_gain, norm2_bias, out_grad,
 ):
-    n_dp, n_t = lax.axis_size("dp"), lax.axis_size("tensor")
-    rows, width = hidden_in.shape
+    n_t = lax.axis_size("tensor")
     cols = w_query.shape[1]
     length = lax.dynamic_slice_in_dim(seq_lengths, lax.axis_index("tensor"), 1)
     packed = jnp.concatenate((w_query, w_key, w_value, w_out), axis=1)
-    whole = gather_all(packed, w_inner, w_outer, n_dp, n_t)
     split = lambda a: a.reshape(n_t, 1, -1)
     zeros = jnp.zeros((n_t, 1, cols), jnp.float32)
     qkv_bias = jnp.concatenate((split(b_query), zeros, split(b_value), zeros), axis=2)
     vec = jnp.stack((b_outer, b_outer, b_out, norm1_gain, norm1_bias, norm2_gain, norm2_bias, b_out))
-    y, grad_in, grads, sums = layer(length, hidden_in, out_grad, whole, qkv_bias, split(b_inner), vec)
-    shards, sums = scatter_all(grads, sums.sum(axis=1), n_dp)
+    y, grad_in, shards, sums = step(
+        length, hidden_in, out_grad, packed, w_inner, w_outer, qkv_bias, split(b_inner), vec, n_t
+    )
     heads = sums[V_BI + n_t :]
     join = lambda a: a.reshape(-1)
     gq, gk, gv, go = (shards[0, :, i * cols : (i + 1) * cols] for i in range(4))

time: 281 us -> 199 us (0.71)
  Pallas kernels: 259 us -> 177 us
    pallas_call x3 -> x1, Pallas kernels: 259 us -> 177 us  [step(): pl.pallas_call(step_kernel, out_shape=(jax.ShapeDtypeStruct((rows, width)...]
where the time goes in v1:
time: 199 us; the launch traced here: 198 us
  Pallas kernels  177 us (89%)
  local copies, waits for them, and re-layouts  18.6 us (9%)
  other arithmetic  2.33 us (1%)
    pallas_call x1, Pallas kernels, step(): pl.pallas_call(step_kernel, out_shape=(jax.ShapeDtypeStruct((rows, width)...  177 us
    another operation x7, local copies, waits for them, and re-layouts, data_parallel(): jnp.stack((b_outer, b_outer, b_out, norm1_gain, norm1_bias, norm2_gain, n...  4.78 us

profile of v1, /device:TPU:0, one launch (start us, length us, event | category | flops | bytes accessed | tf_op | source)
XLA Modules:
  0.0 198.5 jit_solution(3470408342224643371)
XLA Ops:
  0.7 1.2 dynamic_slice.3.length_ref
  1.9 1.6 pad_maximum_fusion.packed_ref
  3.5 0.8 reshape.53
  4.3 0.8 reshape.52
  5.1 0.7 pad_maximum_fusion.1.qkv_bias
  5.8 0.7 stack.23
  6.5 0.7 stack.24
  7.1 0.7 stack.25
  7.8 0.7 stack.26
  8.5 0.7 stack.27
  9.2 0.7 stack.28
  9.9 0.6 stack.29.vec_ref
  10.5 176.9 %shard_map.305 = (bf16[512,768]{1,0:T(8,128)(2,1)}, f32[512,768]{1,0:T(8,128)}, f32[3,96,768]{2,1,0:T(8,128)}, f32[16,768]{1,0:T(8,128)}) custom-call(s32[1]{0:T(128)} %dynamic_slice.3.length_ref, bf16[512,768]{1,0:T(8,128)(2,1)} %x_ref.1, bf16[512,768]{1,0:T(8,128)(2,1)} %og_ref.1, bf16[96,768]{1,0:T(8,128)(2,1)} %pad_maximum_fusion.packed_ref, ...), custom_call_target="tpu_custom_call" | custom-call | tf_op jit(solution)/shard_map/pallas_call | solution.py:901
  187.4 0.0 copy-start.1
  187.5 1.9 slice_bitcast_fusion.2
  189.4 0.0 copy-start
  189.4 0.8 fusion
  190.2 0.7 reshape.55
  190.9 0.7 reshape.56
  191.6 1.6 slice_reduce_fusion
  193.2 1.9 slice_bitcast_fusion
  195.1 0.7 slice.58
  195.8 0.6 reshape.57
  196.4 0.0 copy-done.1
  196.4 0.9 copy.37
  197.3 0.0 copy-done
  197.3 1.1 copy.38
  (1 shorter events, 0.0 us)
Async XLA Ops:
  187.4 9.0 %copy-start.1 = (bf16[512,768]{1,0:T(8,128)(2,1)S(1)}, bf16[512,768]{1,0:T(8,128)(2,1)}, u32[]{:S(2)}) copy-start(bf16[512,768]{1,0:T(8,128)(2,1)} %get-tuple-element.56) | copy-start | bytes 2359300
  189.4 7.9 %copy-start = (f32[512,768]{1,0:T(8,128)S(1)}, f32[512,768]{1,0:T(8,128)}, u32[]{:S(2)}) copy-start(f32[512,768]{1,0:T(8,128)} %get-tuple-element.57) | copy-start | bytes 4718596

commit v2 on v1

--- a/solution.py
+++ b/solution.py
@@ -378,109 +378,170 @@
     )
 
 
-class Gather:
-    def __init__(self, me, shards, w, send_sem, recv_sem, local_sem):
-        self.me, self.shards, self.w = me, shards, w
+def parse(steps):
+    for step in steps:
+        first, _, stop = step[3:].partition("-")
+        for q in range(int(first or 0), int(stop or first or 0) + 1):
+            yield step[0], int(step[1]), q
+
+
+class Routes:
+    def __init__(self, me):
+        self.me = me
+        self.half = me.z // 2
+        self.far = 2 - self.half
+        self.near = 2 * self.half + (1 - me.z % 2)
+        self.mid = (me.z == 1) | (me.z == 2)
+
+    def z_peer(self, z):
+        return {"dp": z * 2 + self.me.x, "tensor": self.me.t}
+
+    def dz_of(self, k):
+        return lax.rem(k * self.half + (4 - k) * (1 - self.half), Z_SIZE)
+
+    def back(self, z):
+        return lax.rem(self.me.z - z + Z_SIZE, Z_SIZE)
+
+
+class Gather(Routes):
+    def __init__(self, me, modes, shards, w, send_sem, recv_sem, local_sem):
+        super().__init__(me)
+        self.modes, self.shards, self.w = modes, shards, w
         self.send_sem, self.recv_sem, self.local_sem = send_sem, recv_sem, local_sem
         self.rows = shards[0].shape[0]
 
-    def block(self, m, chip, core):
-        return block_of(self.w, m, chip[0], chip[1] * 2 + core, self.rows)
-
-    def send(self, m, slot, src, chip, peer):
-        dst = self.block(m, chip, self.me.c)
-        remote(src, dst, self.send_sem.at[m, slot], self.recv_sem.at[m, slot], peer).start()
-
-    def own(self, m, slot, peer):
-        self.send(m, slot, self.shards[m], self.me.chip(0, 0, 0), peer)
-
-    def forward(self, m, slot, dz, da, db, peer):
-        chip = self.me.chip(dz, da, db)
-        self.send(m, slot, self.block(m, chip, self.me.c), chip, peer)
-
-    def slot(self, m, slot):
+    def sem(self, m, send, recv):
         one = block_of(self.w, m, 0, 0, self.rows)
-        return remote(one, one, self.send_sem.at[m, slot], self.recv_sem.at[m, slot], self.me.device(db=1))
+        return remote(one, one, self.send_sem.at[m, send], self.recv_sem.at[m, recv], self.me.device(db=1))
+
+    def wait(self, m, slot):
+        self.sem(m, slot, slot).wait_recv()
+
+    def send(self, m, slot, dz, da, db, peer, own=False, leave=None):
+        dp, y = self.me.chip(dz, da, db)
+        dst = block_of(self.w, m, dp, y * 2 + self.me.c, self.rows)
+        leave = slot if leave is None else leave
+        remote(self.shards[m] if own else dst, dst, self.send_sem.at[m, leave], self.recv_sem.at[m, slot], peer).start()
+
+    def z_slots(self, da):
+        return [(4 * lax.rem(z - self.me.z + Z_SIZE, Z_SIZE) + 2 * da, z) for z in (self.far, self.near)]
+
+    def z_send(self, m, da, own=False):
+        for slot, z in self.z_slots(da):
+            self.send(m, slot, 0, da, 0, self.z_peer(z), own)
 
     def local(self, m):
         me = self.me
-        dst = block_of(self.w, m, me.dp, me.t, self.rows)
-        return pltpu.make_async_copy(self.shards[m], dst, self.local_sem.at[m])
-
-    def begin(self):
+        return pltpu.make_async_copy(self.shards[m], block_of(self.w, m, me.dp, me.t, self.rows), self.local_sem.at[m])
+
+    def place(self, m, q):
+        if self.modes[m] == 0:
+            return q % 4, q // 4
+        return (0, q) if q < 2 else (1 + (q - 2) % 3, (q - 2) // 3)
+
+    def pump(self, m, q):
         me = self.me
-        for m in range(3):
-            for k in range(1, Z_SIZE):
-                self.own(m, k, me.device(dz=Z_SIZE - k))
-            self.own(m, 4, me.device(da=1))
-            self.own(m, 8, me.device(db=1))
-            self.own(m, 16, me.device(other=True))
-            self.local(m).start()
-
-    def pump(self, m, s):
+        k, da = self.place(m, q)
+        dz = self.dz_of(k) if k else 0
+        slot = 4 * dz + 2 * da
+        self.wait(m, slot)
+        if k in (1, 2) and (self.modes[m] == 1 or da == 0):
+
+            @pl.when(self.mid)
+            def _():
+                there = lax.rem(self.near - me.z + dz + Z_SIZE, Z_SIZE)
+                self.send(m, 4 * there + 2 * da, dz, da, 0, self.z_peer(self.near), leave=31 + 2 * da + k)
+
+        if self.modes[m] == 0 and da == 0:
+            self.send(m, 4 * dz + 2, dz, 0, 0, me.device(da=1))
+        if self.modes[m] == 1 and k == 0:
+            self.z_send(m, 1)
+        self.send(m, slot + 1, dz, da, 0, me.device(db=1))
+        self.send(m, 16 + slot, dz, da, 0, me.device(other=True))
+
+    def last(self, m, q):
+        k, da = self.place(m, q)
+        dz = self.dz_of(k) if k else 0
+        slot = 4 * dz + 2 * da + 1
+        self.wait(m, slot)
+        self.send(m, 16 + slot, dz, da, 1, self.me.device(other=True))
+
+    def run(self, steps):
         me = self.me
-        self.slot(m, s).wait_recv()
-
-        @pl.when(s < 4)
-        def _():
-            self.forward(m, 4 + s, s, 0, 0, me.device(da=1))
-            self.forward(m, 8 + 2 * s, s, 0, 0, me.device(db=1))
-            self.forward(m, 16 + 4 * s, s, 0, 0, me.device(other=True))
-
-        @pl.when((s >= 4) & (s < 8))
-        def _():
-            k = s - 4
-            self.forward(m, 9 + 2 * k, k, 1, 0, me.device(db=1))
-            self.forward(m, 18 + 4 * k, k, 1, 0, me.device(other=True))
-
-        @pl.when(s >= 8)
-        def _():
-            k = s - 8
-            self.forward(m, 17 + 2 * k, k // 2, k % 2, 1, me.device(other=True))
-
-    def pumps(self, m, first, last):
-        @pl.loop(first, last)
-        def _(s):
-            self.pump(m, s)
+        for op, m, q in parse(steps):
+            if op == "A":
+                self.send(m, 2, 0, 0, 0, me.device(da=1), True)
+            elif op == "B":
+                self.send(m, 1, 0, 0, 0, me.device(db=1), True)
+                self.send(m, 16, 0, 0, 0, me.device(other=True), True)
+                self.local(m).start()
+            elif op == "y":
+                self.z_send(m, 0, True)
+            elif op == "p":
+                self.pump(m, q)
+            else:
+                self.last(m, q)
 
     def collect(self, m):
         self.local(m).wait()
 
         @pl.loop(16, 32)
         def _(s):
-            self.slot(m, s).wait_recv()
+            self.wait(m, s)
 
     def drain(self):
         for m in range(3):
-
-            @pl.loop(1, 32)
+            left = lambda s: self.sem(m, s, s).wait_send()
+            for da in range(1 + self.modes[m]):
+                for slot, _ in self.z_slots(da):
+                    left(slot)
+
+                @pl.when(self.mid)
+                def _():
+                    left(32 + 2 * da)
+                    left(33 + 2 * da)
+
+            for dz in range(1 if self.modes[m] else Z_SIZE):
+                left(4 * dz + 2)
+
+            @pl.loop(0, 8)
             def _(s):
-                self.slot(m, s).wait_send()
-
-
-class Scatter:
-    def __init__(self, me, w, core_buf, b_buf, a_buf, z_buf, send_sem, recv_sem):
-        self.me, self.w = me, w
-        self.core_buf, self.b_buf, self.a_buf, self.z_buf = core_buf, b_buf, a_buf, z_buf
+                left(2 * s + 1)
+
+            @pl.loop(16, 32)
+            def _(s):
+                left(s)
+
+
+class Scatter(Routes):
+    def __init__(self, me, modes, w, w0_grad, out_ref, core_buf, b_buf, t_buf, send_sem, recv_sem):
+        super().__init__(me)
+        self.out_ref = out_ref
+        self.modes, self.w, self.w0_grad = modes, w, w0_grad
+        self.core_buf, self.b_buf, self.t_buf = core_buf, b_buf, t_buf
         self.send_sem, self.recv_sem = send_sem, recv_sem
-        self.rows = z_buf.shape[2]
+        self.rows = b_buf.shape[2]
 
     def order(self, i):
         me = self.me
-        mine = i // 2
-        core = flip(1 - me.c, mine)
-        return flip(me.y, 1 - i % 2) * 2 + core
+        return flip(me.y, 1 - i // 2) * 2 + flip(1 - me.c, i % 2)
 
     def part(self, m, dz, da, db, core):
         dp, y = self.me.chip(dz, da, db)
+        if m == 0:
+            return self.w0_grad.at[y * 2 + core, pl.ds(pl.multiple_of(dp * self.rows, self.rows), self.rows), :]
         return block_of(self.w, m, dp, y * 2 + core, self.rows)
 
+    def sem(self, m, send, recv):
+        one = self.b_buf.at[m, 0]
+        return remote(one, one, self.send_sem.at[m, send], self.recv_sem.at[m, recv], self.me.device(db=1))
+
     def wait(self, m, slot):
-        one = self.z_buf.at[m, 1]
-        return remote(one, one, self.send_sem.at[m, slot], self.recv_sem.at[m, slot], self.me.device(db=1))
-
-    def go(self, m, slot, src, dst, peer):
-        remote(src, dst, self.send_sem.at[m, slot], self.recv_sem.at[m, slot], peer).start()
+        self.sem(m, slot, slot).wait_recv()
+
+    def go(self, m, slot, src, dst, peer, leave=None):
+        leave = slot if leave is None else leave
+        remote(src, dst, self.send_sem.at[m, leave], self.recv_sem.at[m, slot], peer).start()
 
     def from_core(self, dz, da, db):
         return 4 * dz + 2 * db + da
@@ -488,27 +549,27 @@
     def ready(self, m, i):
         me = self.me
         c = me.c
-        side = 1 - i % 2
-
-        @pl.when(i < 2)
+        side = 1 - i // 2
+
+        def where(s):
+            other = 1 - s // 4
+            return self.dz_of(3 - s % 4), side * (1 - c) + other * c, other * (1 - c) + side * c
+
+        @pl.when(i % 2 == 0)
         def _():
             @pl.loop(0, 8)
             def _(s):
-                dz, other = s // 2, s % 2
-                da = side * (1 - c) + other * c
-                db = other * (1 - c) + side * c
+                dz, da, db = where(s)
                 slot = 4 * dz + 2 * da + db
                 self.go(m, slot, self.part(m, dz, da, db, 1 - c), self.core_buf.at[m, slot], me.device(other=True))
 
-        @pl.when(i >= 2)
+        @pl.when(i % 2 == 1)
         def _():
             @pl.loop(0, 8)
             def _(s):
-                dz, other = s // 2, s % 2
-                da = side * (1 - c) + other * c
-                db = other * (1 - c) + side * c
+                dz, da, db = where(s)
                 slot = self.from_core(dz, da, db)
-                self.wait(m, slot).wait_recv()
+                self.wait(m, slot)
                 self.core_buf[m, slot] = self.part(m, dz, da, db, c)[...] + self.core_buf[m, slot]
 
                 @pl.when(db == 1)
@@ -516,43 +577,100 @@
                     place = 2 * dz + da
                     self.go(m, 16 + place, self.core_buf.at[m, slot], self.b_buf.at[m, place], me.device(db=1))
 
-    def b_step(self, m, k):
-        for da in (1, 0):
-            self.wait(m, 16 + 2 * k + da).wait_recv()
-            self.b_buf[m, 2 * k + da] = self.b_buf[m, 2 * k + da] + self.core_buf[m, self.from_core(k, da, 0)]
-            if da:
-                self.go(m, 24 + k, self.b_buf.at[m, 2 * k + 1], self.a_buf.at[m, k], self.me.device(da=1))
+    def way(self, m, da, j):
+        return 2 * da + j if self.modes[m] else 4 + j
+
+    def end(self, m, da, far):
+        return (4 + 2 * da if self.modes[m] else 6) + far
+
+    def z_out(self, m, dz, da, src):
+        owner = lax.rem(self.me.z - dz + Z_SIZE, Z_SIZE)
+        is_near = owner == self.near
+
+        @pl.when(is_near)
+        def _():
+            j = self.end(m, da, 0)
+            self.go(m, 24 + j, src, self.t_buf.at[m, j], self.z_peer(self.near))
+
+        @pl.when(jnp.logical_not(is_near | self.mid) & (dz != 0))
+        def _():
+            j = self.way(m, da, 0) + (owner != self.far).astype(jnp.int32)
+            self.go(m, 24 + j, src, self.t_buf.at[m, j], self.z_peer(self.near))
+
+    def source(self, m, dz, da):
+        return self.b_buf.at[m, 2 * dz + da] if self.modes[m] else self.t_buf.at[m, dz]
+
+    def b_step(self, m, k, da):
+        dz = self.dz_of(k)
+        place = 2 * dz + da
+        self.wait(m, 16 + place)
+        self.b_buf[m, place] = self.b_buf[m, place] + self.core_buf[m, self.from_core(dz, da, 0)]
+        if self.modes[m] == 1:
+            self.z_out(m, dz, da, self.b_buf.at[m, place])
+        elif da == 1:
+            self.go(m, 24 + dz, self.b_buf.at[m, place], self.t_buf.at[m, dz], self.me.device(da=1))
 
     def a_step(self, m, k):
-        self.wait(m, 24 + k).wait_recv()
-        self.a_buf[m, k] = self.a_buf[m, k] + self.b_buf[m, 2 * k]
-
-        @pl.when(k > 0)
+        dz = self.dz_of(k)
+        self.wait(m, 24 + dz)
+        self.t_buf[m, dz] = self.t_buf[m, dz] + self.b_buf[m, 2 * dz]
+        self.z_out(m, dz, 0, self.t_buf.at[m, dz])
+
+    def z_step(self, m, da, j):
+        @pl.when(self.mid)
         def _():
-            self.go(m, 28 + k, self.a_buf.at[m, k], self.z_buf.at[m, k], self.me.device(dz=k))
-
-    def steps(self, step, m):
-        @pl.loop(0, Z_SIZE)
-        def _(k):
-            step(m, k)
-
-    def finish(self, m, out_ref):
-        total = self.a_buf[m, 0].astype(jnp.float32)
-        for k in range(1, Z_SIZE):
-            self.wait(m, 28 + k).wait_recv()
-            total = total + self.z_buf[m, k].astype(jnp.float32)
-        out_ref[m] = total
+            owner = flip(self.far % 2, j) + 2 * (1 - self.half)
+            way, end = self.way(m, da, j), self.end(m, da, 1)
+            self.wait(m, 24 + way)
+            self.t_buf[m, way] = self.t_buf[m, way] + self.source(m, self.back(owner), da)[...]
+            self.go(m, 24 + end, self.t_buf.at[m, way], self.t_buf.at[m, end], self.z_peer(owner), leave=24 + way)
+
+    def last_step(self, m):
+        near, far = self.end(m, 1, 0), self.end(m, 1, 1)
+        self.wait(m, 24 + near)
+        self.wait(m, 24 + far)
+        self.t_buf[m, near] = self.t_buf[m, near] + self.t_buf[m, far] + self.b_buf[m, 1]
+        self.go(m, 32, self.t_buf.at[m, near], self.t_buf.at[m, 8], self.me.device(da=1))
+
+    def run(self, steps):
+        for op, m, q in parse(steps):
+            if op == "b":
+                self.b_step(m, 3 - q // 2, 1 - q % 2)
+            elif op == "c":
+                self.b_step(m, 3 - q % 4, 1 - q // 4)
+            elif op == "a":
+                self.a_step(m, 3 - q)
+            elif op == "z":
+                self.z_step(m, (1 - q // 2) * self.modes[m], 1 - q % 2)
+            elif op == "e":
+                self.last_step(m)
+            else:
+                self.finish(m)
+
+    def finish(self, m):
+        wide = lambda ref: ref[...].astype(jnp.float32)
+        near = self.end(m, 0, 0)
+        self.wait(m, 24 + near)
+        self.wait(m, 25 + near)
+        total = wide(self.source(m, 0, 0)) + wide(self.t_buf.at[m, near]) + wide(self.t_buf.at[m, near + 1])
+        if self.modes[m] == 1:
+            self.wait(m, 32)
+            total = total + wide(self.t_buf.at[m, 8])
+        self.out_ref[m] = total
 
     def drain(self):
         for m in range(3):
-
-            @pl.loop(0, 28)
+            left = lambda s: self.sem(m, s, s).wait_send()
+
+            @pl.loop(0, 24)
             def _(s):
-                self.wait(m, s).wait_send()
-
-            @pl.loop(29, 32)
-            def _(s):
-                self.wait(m, s).wait_send()
+                left(s)
+
+            for da in range(1 + self.modes[m]):
+                for j in (self.way(m, da, 0), self.way(m, da, 1), self.end(m, da, 0)):
+                    left(24 + j)
+            for j in (8,) if self.modes[m] else range(Z_SIZE):
+                left(24 + j)
 
 
 class VectorSum:
@@ -767,65 +885,111 @@
             self.piece(t, 0, j)[...] = low((dot_tn(k, ds) * scale).T)
             between(j)
 
+    def head_sums(self, t):
+        def body(r):
+            self.sums[V_BI + self.n_t + t] += fold(self.qkv[t, r, :].astype(jnp.float32))
+
+        self.tiles(body)
+
+    def project_grad(self, t):
+        self.w0_grad[t] = low(dot_nn(self.x_t[...], self.qkv[t]))
+        out = self.w0_grad.at[t, :, self.ocol :]
+        out[...] = low(out[...].astype(jnp.float32) + dot_nn(self.df_t[...], self.att[t]))
+
     def project_back(self, t):
         self.acc[...] += dot_nt(self.qkv[t], self.w[0, t])
 
-        def body(r):
-            self.sums[V_BI + self.n_t + t] += fold(self.qkv[t, r, :].astype(jnp.float32))
-
-        self.tiles(body)
-        self.w[0, t] = low(dot_nn(self.x_t[...], self.qkv[t]))
-        out = self.w.at[0, t, :, self.ocol :]
-        out[...] = low(out[...].astype(jnp.float32) + dot_nn(self.df_t[...], self.att[t]))
-
     def transpose(self, src, dst):
         dst[...] = src[...].T
 
 
 def fold(a):
     return jnp.sum(a.reshape(a.shape[0] // 8, 8, a.shape[1]), axis=0)
+
+
+GATHER_MODES = (0, 1, 1)
+SCATTER_MODES = (0, 1, 1)
+GATHER_MODES = (0, 1, 1)
+SCATTER_MODES = (0, 1, 1)
+GATHER = {
+    "first": ("A0:0", "y0:0", "B1:0"),
+    "start": ("B0:0", "A2:0", "A1:0", "y1:0", "p0:4", "p0:1", "l0:0", "p0:2", "p1:2", "y2:0", "l0:1", "p0:5", "l0:4", "p0:3",
+        "p0:6-7", "p1:1", "l0:5", "l1:2", "p2:2", "l0:6", "p2:1", "p1:5", "l0:3", "l0:2", "l0:7", "p1:3"),
+    "attend": (),
+    "heads": {3: ("l1:0",), 4: ("l1:5", "l1:1"), 5: ("l2:2", "p1:6"), 6: ("p1:4", "p2:5"), 8: ("l1:6", "l1:3"), 9: ("p2:3",),
+        10: ("l1:4", "l2:0"), 11: ("p2:6",)},
+    "out": {1: ("B2:0",), 2: ("l2:1", "p1:7"), 3: ("l1:7",)},
+    "norm": ("p2:4",),
+    "ffn": ("l2:6",),
+    "inner": {0: ("p2:7",), 2: ("l2:4", "l2:3", "l2:5", "l2:7")},
+}
+SCATTER = {
+    "outer": {},
+    "inner": {0: ("b2:0",), 1: ("b2:2",), 2: ("b2:1", "z2:0", "b2:4", "b2:3")},
+    "norm": ("b2:5",),
+    "heads": {0: ("b1:2",), 2: ("z2:2", "b1:0"), 5: ("z2:3", "b2:6", "b1:1"), 7: ("b1:3", "b1:6"), 8: ("z1:1",), 9:
+        ("e2:0",), 10: ("z1:0",)},
+    "grad": {0: ("b1:4",), 1: ("z2:1",), 3: ("b0:0", "b1:7", "z1:2", "b0:2", "b1:5", "b0:4", "b0:1")},
+    "last": ((), (), ("e1:0", "z1:3", "b0:6", "b0:3", "a0:0", "b0:5", "a0:1", "z0:0", "a0:2", "z0:1", "b0:7"), ("b2:7",
+        "F2:0", "a0:3", "F1:0", "F0:0")),
+}
 
 
 def step_kernel(
     length_ref, x_ref, og_ref, packed_ref, wi_ref, wo_ref, qkv_bias, inner_bias, vec_ref,
     y_ref, acc_ref, out_ref, vout_ref,
-    w, sums, qkv, p, att, z1, inv1, h1b, act, slope, df, datt, dact, x_t, h1b_t, df_t,
-    core_buf, b_buf, a_buf, z_buf, vec_buf, vec_z,
+    w, sums, qkv, p, att, z1, inv1, h1b, ffn, df, datt, dact, x_t, h1b_t, df_t,
+    core_buf, b_buf, t_buf, vec_buf, vec_z,
     gather_send, gather_recv, local_sem, send_sem, recv_sem, vec_send, vec_recv,
 ):
     me = Place()
-    gather = Gather(me, (packed_ref, wi_ref, wo_ref), w, gather_send, gather_recv, local_sem)
-    scatter = Scatter(me, w, core_buf, b_buf, a_buf, z_buf, send_sem, recv_sem)
+    rows, width = x_ref.shape
+    act, slope, w0_grad = ffn.at[:, :rows], ffn.at[:, rows:], ffn.at[:, :width]
+    gather = Gather(me, GATHER_MODES, (packed_ref, wi_ref, wo_ref), w, gather_send, gather_recv, local_sem)
+    scatter = Scatter(me, SCATTER_MODES, w, w0_grad, out_ref, core_buf, b_buf, t_buf, send_sem, recv_sem)
     small = VectorSum(me, vec_buf, vec_z, vec_send, vec_recv)
+    a = Layer(
+        x=x_ref, og=og_ref, w=w, w0_grad=w0_grad, qkv_bias=qkv_bias, inner_bias=inner_bias, vec=vec_ref, y=y_ref, acc=acc_ref, sums=sums,
+        qkv=qkv, p=p, att=att, z1=z1, inv1=inv1, h1b=h1b, act=act, slope=slope, df=df, datt=datt, dact=dact, x_t=x_t, h1b_t=h1b_t, df_t=df_t,
+    )
+
+    def at(run, slots, i):
+        for n, steps in slots.items():
+
+            @pl.when(i == n)
+            def _():
+                run(steps)
+
+    def heads(run, slots, i, j):
+        at(run, {n // a.heads: steps for n, steps in slots.items() if n % a.heads == j}, i)
+
     meet(me)
-    gather.begin()
-    a = Layer(
-        x=x_ref, og=og_ref, w=w, qkv_bias=qkv_bias, inner_bias=inner_bias, vec=vec_ref, y=y_ref, acc=acc_ref, sums=sums,
-        qkv=qkv, p=p, att=att, z1=z1, inv1=inv1, h1b=h1b, act=act, slope=slope, df=df, datt=datt, dact=dact, x_t=x_t, h1b_t=h1b_t, df_t=df_t,
-    )
+    gather.run(GATHER["first"])
     length = length_ref[0]
     valid = lax.broadcasted_iota(jnp.int32, (a.rows, 1), 0) < length
     a.transpose(a.x, a.x_t)
     a.start_residual()
-    gather.pumps(0, 1, 16)
+    gather.run(GATHER["start"])
     gather.collect(0)
+    gather.run(GATHER["attend"])
 
     @pl.loop(0, a.n_t)
     def _(t):
         a.project(t)
-        a.attend(t, valid, lambda j: gather.pump(1, a.heads * t + j + 1))
+        a.attend(t, valid, lambda j: heads(gather.run, GATHER["heads"], t, j))
         a.out_project(t)
-
-    gather.pumps(1, 1 + a.n_t * a.heads, 16)
+        at(gather.run, GATHER["out"], t)
+
     a.first_norm()
     a.transpose(a.h1b, a.h1b_t)
-    gather.pumps(2, 1, 4)
+    gather.run(GATHER["norm"])
     gather.collect(1)
+    gather.run(GATHER["ffn"])
 
     @pl.loop(0, a.n_t)
     def _(t):
-        gather.pumps(2, 4 + 3 * t, 7 + 3 * t)
         a.inner(t)
+        at(gather.run, GATHER["inner"], t)
 
     gather.collect(2)
 
@@ -841,48 +1005,43 @@
     def _(i):
         a.outer_back(scatter.order(i))
         scatter.ready(2, i)
+        at(scatter.run, SCATTER["outer"], i)
 
     @pl.loop(0, a.n_t)
     def _(i):
         a.inner_back(scatter.order(i))
         scatter.ready(1, i)
+        at(scatter.run, SCATTER["inner"], i)
 
     a.first_norm_back()
     a.transpose(a.df, a.df_t)
-
-    def between(i, j):
-        n = a.heads * i + j
-
-        @pl.when(n < 4)
-        def _():
-            scatter.b_step(2, n)
-
-        @pl.when((n >= 4) & (n < 8))
-        def _():
-            scatter.a_step(2, n - 4)
-
-        @pl.when((n >= 6) & (n < 10))
-        def _():
-            scatter.b_step(1, n - 6)
+    scatter.run(SCATTER["norm"])
 
     @pl.loop(0, a.n_t)
     def _(i):
         t = scatter.order(i)
-        a.attend_back(t, lambda j: between(i, j))
+        a.attend_back(t, lambda j: heads(scatter.run, SCATTER["heads"], i, j))
+        a.head_sums(t)
+
+        @pl.when(i == a.n_t - 1)
+        def _():
+            small.start(jnp.sum(sums[...], axis=1))
+
+        a.project_grad(t)
+
+        @pl.when(i == a.n_t - 1)
+        def _():
+            small.advance(0)
+
+        scatter.ready(0, i)
+        at(scatter.run, SCATTER["grad"], i)
+
+    for t, steps in enumerate(SCATTER["last"]):
         a.project_back(t)
-        scatter.ready(0, i)
-
-    small.start(jnp.sum(sums[...], axis=1))
-    scatter.steps(scatter.a_step, 1)
-    small.advance(0)
-    scatter.steps(scatter.b_step, 0)
-    small.advance(1)
-    scatter.steps(scatter.a_step, 0)
-    small.advance(2)
-    for m in (2, 1):
-        scatter.finish(m, out_ref)
+        if t in (1, 3):
+            small.advance((t + 1) // 2)
+        scatter.run(steps)
     vout_ref[...] = small.result()
-    scatter.finish(0, out_ref)
     scatter.drain()
 
 
@@ -917,8 +1076,7 @@
             pltpu.VMEM((rows, width), f32),
             pltpu.VMEM((rows, 128), f32),
             pltpu.VMEM((rows, width), bf),
-            pltpu.VMEM((n_t, rows, width), bf),
-            pltpu.VMEM((n_t, rows, width), bf),
+            pltpu.VMEM((n_t, max(2 * rows, width), width), bf),
             pltpu.VMEM((rows, width), bf),
             pltpu.VMEM((rows, owidth), bf),
             pltpu.VMEM((rows, width), f32),
@@ -927,15 +1085,14 @@
             pltpu.VMEM((width, rows), bf),
             buf(16),
             buf(8),
-            buf(4),
-            buf(4),
+            buf(9),
             pltpu.VMEM((7, n_v, width), f32),
             pltpu.VMEM((Z_SIZE, n_v, width), f32),
-            dma((3, 32)),
-            dma((3, 32)),
+            dma((3, 36)),
+            dma((3, 36)),
             dma((3,)),
-            dma((3, 32)),
-            dma((3, 32)),
+            dma((3, 33)),
+            dma((3, 33)),
             dma((6,)),
             dma((6,)),
         ],

time: 199 us -> 169 us (0.85)
  Pallas kernels: 177 us -> 147 us
    pallas_call x1, Pallas kernels: 177 us -> 147 us  [step(): pl.pallas_call(step_kernel, out_shape=(jax.ShapeDtypeStruct((rows, width)...]
where the time goes in v2:
time: 169 us; the launch traced here: 168 us
  Pallas kernels  147 us (87%)
  local copies, waits for them, and re-layouts  18.6 us (11%)
  other arithmetic  2.33 us (1%)
    pallas_call x1, Pallas kernels, step(): pl.pallas_call(step_kernel, out_shape=(jax.ShapeDtypeStruct((rows, width)...  147 us
    another operation x7, local copies, waits for them, and re-layouts, data_parallel(): jnp.stack((b_outer, b_outer, b_out, norm1_gain, norm1_bias, norm2_gain, n...  4.78 us

profile of v2, /device:TPU:0, one launch (start us, length us, event | category | flops | bytes accessed | tf_op | source)
XLA Modules:
  0.0 168.1 jit_solution(7676910917463826229)
XLA Ops:
  0.7 1.2 dynamic_slice.3.length_ref
  1.9 1.6 pad_maximum_fusion.packed_ref
  3.5 0.8 reshape.53
  4.3 0.8 reshape.52
  5.1 0.7 pad_maximum_fusion.1.qkv_bias
  5.8 0.7 stack.23
  6.5 0.7 stack.24
  7.1 0.7 stack.25
  7.8 0.7 stack.26
  8.5 0.7 stack.27
  9.2 0.7 stack.28
  9.9 0.6 stack.29.vec_ref
  10.5 146.5 %shard_map.305 = (bf16[512,768]{1,0:T(8,128)(2,1)}, f32[512,768]{1,0:T(8,128)}, f32[3,96,768]{2,1,0:T(8,128)}, f32[16,768]{1,0:T(8,128)}) custom-call(s32[1]{0:T(128)} %dynamic_slice.3.length_ref, bf16[512,768]{1,0:T(8,128)(2,1)} %x_ref.1, bf16[512,768]{1,0:T(8,128)(2,1)} %og_ref.1, bf16[96,768]{1,0:T(8,128)(2,1)} %pad_maximum_fusion.packed_ref, ...), custom_call_target="tpu_custom_call" | custom-call | tf_op jit(solution)/shard_map/pallas_call | solution.py:1060
  157.1 0.0 copy-start.1
  157.1 1.9 %slice_bitcast_fusion.2 = (f32[96,192]{1,0:T(8,128)}, f32[96,192]{1,0:T(8,128)}, f32[96,192]{1,0:T(8,128)}, f32[96,192]{1,0:T(8,128)}) fusion(f32[3,96,768]{2,1,0:T(8,128)} %get-tuple-element.23), kind=kLoop, calls=%fused_computation.3 | loop fusion | bytes 589824 | tf_op jit(solution)/shard_map/squeeze | solution.py:1120
  159.0 0.0 copy-start
  159.0 0.8 fusion
  159.8 0.7 reshape.55
  160.5 0.7 reshape.56
  161.2 1.6 slice_reduce_fusion
  162.8 1.9 %slice_bitcast_fusion = (f32[96,768]{1,0:T(8,128)}, f32[96,768]{1,0:T(8,128)}) fusion(f32[3,96,768]{2,1,0:T(8,128)} %get-tuple-element.23), kind=kLoop, calls=%fused_computation | loop fusion | bytes 1179648 | tf_op jit(solution)/shard_map/squeeze | solution.py:1123
  164.7 0.7 slice.58
  165.4 0.6 reshape.57
  166.1 0.0 copy-done.1
  166.1 0.9 copy.37
  166.9 0.0 copy-done
  166.9 1.1 copy.38
  (1 shorter events, 0.0 us)
Async XLA Ops:
  157.1 9.0 %copy-start.1 = (bf16[512,768]{1,0:T(8,128)(2,1)S(1)}, bf16[512,768]{1,0:T(8,128)(2,1)}, u32[]{:S(2)}) copy-start(bf16[512,768]{1,0:T(8,128)(2,1)} %get-tuple-element.56) | copy-start | bytes 2359300
  159.0 7.9 %copy-start = (f32[512,768]{1,0:T(8,128)S(1)}, f32[512,768]{1,0:T(8,128)}, u32[]{:S(2)}) copy-start(f32[512,768]{1,0:T(8,128)} %get-tuple-element.57) | copy-start | bytes 4718596

commit v3 on v2

--- a/solution.py
+++ b/solution.py
@@ -363,13 +363,17 @@
     return ref.at[m, t, pl.ds(pl.multiple_of(dp * rows, rows), rows), :]
 
 
+def peers_of(me):
+    return [me.device(dz=k) for k in range(1, Z_SIZE)] + [me.device(da=1), me.device(db=1), me.device(other=True)]
+
+
+def greet(me):
+    for peer in peers_of(me):
+        pl.semaphore_signal(pltpu.get_barrier_semaphore(), inc=1, device_id=peer, device_id_type=MESH_IDS)
+
+
 def meet(me):
-    barrier = pltpu.get_barrier_semaphore()
-    peers = [me.device(dz=k) for k in range(1, Z_SIZE)]
-    peers += [me.device(da=1), me.device(db=1), me.device(other=True)]
-    for peer in peers:
-        pl.semaphore_signal(barrier, inc=1, device_id=peer, device_id_type=MESH_IDS)
-    pl.semaphore_wait(barrier, len(peers))
+    pl.semaphore_wait(pltpu.get_barrier_semaphore(), len(peers_of(me)))
 
 
 def remote(src, dst, send, recv, peer):
@@ -404,11 +408,11 @@
 
 
 class Gather(Routes):
-    def __init__(self, me, modes, shards, w, send_sem, recv_sem, local_sem):
+    def __init__(self, me, modes, w, send_sem, recv_sem):
         super().__init__(me)
-        self.modes, self.shards, self.w = modes, shards, w
-        self.send_sem, self.recv_sem, self.local_sem = send_sem, recv_sem, local_sem
-        self.rows = shards[0].shape[0]
+        self.modes, self.w = modes, w
+        self.send_sem, self.recv_sem = send_sem, recv_sem
+        self.rows = w.shape[2] // lax.axis_size("dp")
 
     def sem(self, m, send, recv):
         one = block_of(self.w, m, 0, 0, self.rows)
@@ -417,22 +421,21 @@
     def wait(self, m, slot):
         self.sem(m, slot, slot).wait_recv()
 
-    def send(self, m, slot, dz, da, db, peer, own=False, leave=None):
+    def send(self, m, slot, dz, da, db, peer, leave=None):
         dp, y = self.me.chip(dz, da, db)
         dst = block_of(self.w, m, dp, y * 2 + self.me.c, self.rows)
         leave = slot if leave is None else leave
-        remote(self.shards[m] if own else dst, dst, self.send_sem.at[m, leave], self.recv_sem.at[m, slot], peer).start()
+        remote(dst, dst, self.send_sem.at[m, leave], self.recv_sem.at[m, slot], peer).start()
 
     def z_slots(self, da):
         return [(4 * lax.rem(z - self.me.z + Z_SIZE, Z_SIZE) + 2 * da, z) for z in (self.far, self.near)]
 
-    def z_send(self, m, da, own=False):
+    def z_send(self, m, da):
         for slot, z in self.z_slots(da):
-            self.send(m, slot, 0, da, 0, self.z_peer(z), own)
-
-    def local(self, m):
-        me = self.me
-        return pltpu.make_async_copy(self.shards[m], block_of(self.w, m, me.dp, me.t, self.rows), self.local_sem.at[m])
+            self.send(m, slot, 0, da, 0, self.z_peer(z))
+
+    def own(self, m):
+        return block_of(self.w, m, self.me.dp, self.me.t, self.rows)
 
     def place(self, m, q):
         if self.modes[m] == 0:
@@ -470,21 +473,18 @@
         me = self.me
         for op, m, q in parse(steps):
             if op == "A":
-                self.send(m, 2, 0, 0, 0, me.device(da=1), True)
+                self.send(m, 2, 0, 0, 0, me.device(da=1))
             elif op == "B":
-                self.send(m, 1, 0, 0, 0, me.device(db=1), True)
-                self.send(m, 16, 0, 0, 0, me.device(other=True), True)
-                self.local(m).start()
+                self.send(m, 1, 0, 0, 0, me.device(db=1))
+                self.send(m, 16, 0, 0, 0, me.device(other=True))
             elif op == "y":
-                self.z_send(m, 0, True)
+                self.z_send(m, 0)
             elif op == "p":
                 self.pump(m, q)
             else:
                 self.last(m, q)
 
     def collect(self, m):
-        self.local(m).wait()
-
         @pl.loop(16, 32)
         def _(s):
             self.wait(m, s)
@@ -936,22 +936,30 @@
 
 
 def step_kernel(
-    length_ref, x_ref, og_ref, packed_ref, wi_ref, wo_ref, qkv_bias, inner_bias, vec_ref,
+    length_ref, x_in, og_in, wq, wk, wv, wo, w_inner, w_outer, b_outer, b_value, b_out, gain1, bias1, gain2, bias2, b_query, b_inner,
     y_ref, acc_ref, out_ref, vout_ref,
+    x_ref, og_ref, parts, vec_ref, qkv_bias, inner_bias,
     w, sums, qkv, p, att, z1, inv1, h1b, ffn, df, datt, dact, x_t, h1b_t, df_t,
     core_buf, b_buf, t_buf, vec_buf, vec_z,
-    gather_send, gather_recv, local_sem, send_sem, recv_sem, vec_send, vec_recv,
+    load_sem, gather_send, gather_recv, send_sem, recv_sem, vec_send, vec_recv,
 ):
     me = Place()
     rows, width = x_ref.shape
     act, slope, w0_grad = ffn.at[:, :rows], ffn.at[:, rows:], ffn.at[:, :width]
-    gather = Gather(me, GATHER_MODES, (packed_ref, wi_ref, wo_ref), w, gather_send, gather_recv, local_sem)
+    gather = Gather(me, GATHER_MODES, w, gather_send, gather_recv)
     scatter = Scatter(me, SCATTER_MODES, w, w0_grad, out_ref, core_buf, b_buf, t_buf, send_sem, recv_sem)
     small = VectorSum(me, vec_buf, vec_z, vec_send, vec_recv)
     a = Layer(
         x=x_ref, og=og_ref, w=w, w0_grad=w0_grad, qkv_bias=qkv_bias, inner_bias=inner_bias, vec=vec_ref, y=y_ref, acc=acc_ref, sums=sums,
         qkv=qkv, p=p, att=att, z1=z1, inv1=inv1, h1b=h1b, act=act, slope=slope, df=df, datt=datt, dact=dact, x_t=x_t, h1b_t=h1b_t, df_t=df_t,
     )
+    vectors = (b_outer, b_value, b_out, gain1, bias1, gain2, bias2, b_query)
+    pairs = [(ref, parts.at[i]) for i, ref in enumerate((wq, wk, wv, wo))]
+    pairs += [(w_inner, gather.own(1)), (w_outer, gather.own(2)), (x_in, x_ref), (b_inner, inner_bias)]
+    pairs += [(ref, vec_ref.at[i]) for i, ref in enumerate(vectors)] + [(og_in, og_ref)]
+    loads = [pltpu.make_async_copy(src, dst, load_sem.at[i]) for i, (src, dst) in enumerate(pairs)]
+    for load in loads:
+        load.start()
 
     def at(run, slots, i):
         for n, steps in slots.items():
@@ -963,9 +971,22 @@
     def heads(run, slots, i, j):
         at(run, {n // a.heads: steps for n, steps in slots.items() if n % a.heads == j}, i)
 
+    greet(me)
+    for load in loads[:6]:
+        load.wait()
+    packed = gather.own(0)
+    for i in range(4):
+        packed[:, i * a.cols : (i + 1) * a.cols] = parts[i]
     meet(me)
     gather.run(GATHER["first"])
-    length = length_ref[0]
+    for load in loads[6:]:
+        load.wait()
+    for t in range(a.n_t):
+        here = slice(t * a.cols, (t + 1) * a.cols)
+        qkv_bias[t] = jnp.zeros((1, width), jnp.float32)
+        qkv_bias[t, :, : a.cols] = vec_ref[7:8, here]
+        qkv_bias[t, :, 2 * a.cols : 3 * a.cols] = vec_ref[1:2, here]
+    length = length_ref[me.t]
     valid = lax.broadcasted_iota(jnp.int32, (a.rows, 1), 0) < length
     a.transpose(a.x, a.x_t)
     a.start_residual()
@@ -1045,18 +1066,19 @@
     scatter.drain()
 
 
-def step(length, x, og, packed, inner, outer, qkv_bias, inner_bias, vec, n_t):
+def step(seq_lengths, x, og, weights, vectors, b_inner, n_t):
     rows, width = x.shape
     cols = width // n_t
     heads = width // HEAD_DIM
     owidth = width - (3 * cols) // 128 * 128
-    shard = packed.shape[0]
+    shard = weights[0].shape[0]
     bf, f32 = jnp.bfloat16, jnp.float32
-    vmem = pl.BlockSpec(memory_space=pltpu.VMEM)
+    vmem, anywhere = pl.BlockSpec(memory_space=pltpu.VMEM), pl.BlockSpec(memory_space=pl.ANY)
     n_v = V_BI + 2 * n_t
     n_w = shard * lax.axis_size("dp")
     buf = lambda n: pltpu.VMEM((3, n, shard, width), bf)
     dma = pltpu.SemaphoreType.DMA
+    n_loads = 3 + len(weights) + len(vectors)
     return pl.pallas_call(
         step_kernel,
         out_shape=(
@@ -1065,9 +1087,15 @@
             jax.ShapeDtypeStruct((3, shard, width), f32),
             jax.ShapeDtypeStruct((n_v, width), f32),
         ),
-        in_specs=[pl.BlockSpec(memory_space=pltpu.SMEM)] + [vmem] * 8,
+        in_specs=[pl.BlockSpec(memory_space=pltpu.SMEM)] + [anywhere] * n_loads,
         out_specs=[vmem] * 4,
         scratch_shapes=[
+            pltpu.VMEM((rows, width), bf),
+            pltpu.VMEM((rows, width), bf),
+            pltpu.VMEM((4, shard, cols), bf),
+            pltpu.VMEM((len(vectors), width), f32),
+            pltpu.VMEM((n_t, 1, width), f32),
+            pltpu.VMEM((n_t, 1, width), f32),
             pltpu.VMEM((3, n_t, n_w, width), bf),
             pltpu.VMEM((n_v, 8, width), f32),
             pltpu.VMEM((n_t, rows, width), bf),
@@ -1088,16 +1116,61 @@
             buf(9),
             pltpu.VMEM((7, n_v, width), f32),
             pltpu.VMEM((Z_SIZE, n_v, width), f32),
+            dma((n_loads,)),
             dma((3, 36)),
             dma((3, 36)),
-            dma((3,)),
             dma((3, 33)),
             dma((3, 33)),
             dma((6,)),
             dma((6,)),
         ],
         compiler_params=pltpu.CompilerParams(collective_id=0, has_side_effects=True, vmem_limit_bytes=63 * 2**20),
-    )(length, x, og, packed, inner, outer, qkv_bias, inner_bias, vec)
+    )(seq_lengths, x, og, *weights, *vectors, b_inner)
+
+
+def place_kernel(n_t, y_in, gin_in, shards, sums, y, gin, gq, gk, gv, go, gi, gf, bq, bv, bo, g1, b1, bi, bf, g2, b2, y_buf, gin_buf, sems):
+    first = [pltpu.make_async_copy(y_in, y_buf, sems.at[0]), pltpu.make_async_copy(gin_in, gin_buf, sems.at[1])]
+    then = [pltpu.make_async_copy(y_buf, y, sems.at[2]), pltpu.make_async_copy(gin_buf, gin, sems.at[3])]
+    direct = [pltpu.make_async_copy(shards.at[i], ref, sems.at[3 + i]) for i, ref in ((1, gi), (2, gf))]
+    for copy in first + direct:
+        copy.start()
+    cols = gq.shape[1]
+    for i, ref in enumerate((gq, gk, gv, go)):
+        ref[...] = shards[0, :, i * cols : (i + 1) * cols]
+    for row, ref in ((V_BO, bo), (V_G1, g1), (V_B1, b1), (V_BF, bf), (V_G2, g2), (V_B2, b2)):
+        ref[...] = sums[row : row + 1, :].reshape(ref.shape)
+    for t in range(n_t):
+        bi[t] = sums[V_BI + t : V_BI + t + 1, :]
+    heads = [sums[V_BI + n_t + t : V_BI + n_t + t + 1, :] for t in range(n_t)]
+    bq[...] = jnp.concatenate([h[:, :cols] for h in heads], axis=1).reshape(bq.shape)
+    bv[...] = jnp.concatenate([h[:, 2 * cols : 3 * cols] for h in heads], axis=1).reshape(bv.shape)
+    for copy, after in zip(first, then):
+        copy.wait()
+        after.start()
+    for copy in direct + then:
+        copy.wait()
+
+
+def place(y, gin, shards, sums, n_t):
+    shard, width = shards.shape[1:]
+    cols = width // n_t
+    f32 = jnp.float32
+    vmem, anywhere = pl.BlockSpec(memory_space=pltpu.VMEM), pl.BlockSpec(memory_space=pl.ANY)
+    row = jax.ShapeDtypeStruct((width,), f32)
+    return pl.pallas_call(
+        functools.partial(place_kernel, n_t),
+        out_shape=(
+            [jax.ShapeDtypeStruct(y.shape, y.dtype), jax.ShapeDtypeStruct(gin.shape, f32)]
+            + [jax.ShapeDtypeStruct((shard, cols), f32)] * 4
+            + [jax.ShapeDtypeStruct((shard, width), f32)] * 2
+            + [row] * 5
+            + [jax.ShapeDtypeStruct((n_t, 1, width), f32)]
+            + [row] * 3
+        ),
+        in_specs=[anywhere, anywhere, vmem, vmem],
+        out_specs=[anywhere] * 2 + [vmem] * 4 + [anywhere] * 2 + [vmem] * 9,
+        scratch_shapes=[pltpu.VMEM(y.shape, y.dtype), pltpu.VMEM(gin.shape, f32), pltpu.SemaphoreType.DMA((6,))],
+    )(y, gin, shards, sums)
 
 
 def data_parallel(
@@ -1105,23 +1178,13 @@
     w_inner, b_inner, w_outer, b_outer, norm2_gain, norm2_bias, out_grad,
 ):
     n_t = lax.axis_size("tensor")
-    cols = w_query.shape[1]
-    length = lax.dynamic_slice_in_dim(seq_lengths, lax.axis_index("tensor"), 1)
-    packed = jnp.concatenate((w_query, w_key, w_value, w_out), axis=1)
-    split = lambda a: a.reshape(n_t, 1, -1)
-    zeros = jnp.zeros((n_t, 1, cols), jnp.float32)
-    qkv_bias = jnp.concatenate((split(b_query), zeros, split(b_value), zeros), axis=2)
-    vec = jnp.stack((b_outer, b_outer, b_out, norm1_gain, norm1_bias, norm2_gain, norm2_bias, b_out))
-    y, grad_in, shards, sums = step(
-        length, hidden_in, out_grad, packed, w_inner, w_outer, qkv_bias, split(b_inner), vec, n_t
-    )
-    heads = sums[V_BI + n_t :]
-    join = lambda a: a.reshape(-1)
-    gq, gk, gv, go = (shards[0, :, i * cols : (i + 1) * cols] for i in range(4))
-    return (
-        y, grad_in, gq, join(heads[:, :cols]), gk, gv, join(heads[:, 2 * cols : 3 * cols]), go, sums[V_BO], sums[V_G1], sums[V_B1],
-        shards[1], join(sums[V_BI : V_BI + n_t]), shards[2], sums[V_BF], sums[V_G2], sums[V_B2],
-    )
+    width = hidden_in.shape[1]
+    vectors = (b_outer, b_value, b_out, norm1_gain, norm1_bias, norm2_gain, norm2_bias, b_query)
+    weights = (w_query, w_key, w_value, w_out, w_inner, w_outer)
+    done = step(seq_lengths, hidden_in, out_grad, weights, vectors, b_inner.reshape(n_t, 1, width), n_t)
+    y, gin, gq, gk, gv, go, gi, gf, *small = place(*done, n_t)
+    bq, bv, bo, g1, b1, bi, bf, g2, b2 = small
+    return y, gin, gq, bq, gk, gv, bv, go, bo, g1, b1, gi, bi.reshape(-1), gf, bf, g2, b2
 
 
 def solution(mesh):

time: 169 us -> 151 us (0.89)
  local copies, waits for them, and re-layouts: 18.6 us -> 0 us
  Pallas kernels: 147 us -> 150 us
  other arithmetic: 2.33 us -> 0 us
    pallas_call x0 -> x1, Pallas kernels: none -> 5.01 us  [place(): pl.pallas_call(functools.partial(place_kernel, n_t), out_shape=[jax.Shape...]
    another operation x7 -> x0, local copies, waits for them, and re-layouts: 4.78 us -> none  [data_parallel(): jnp.stack((b_outer, b_outer, b_out, norm1_gain, norm1_bias, norm2_gain, n...]
    squeeze x2 -> x0, local copies, waits for them, and re-layouts: 3.83 us -> none  [the longest x1 1.93 us: data_parallel(): gq, gk, gv, go = (shards[0, :, i * cols:(i + 1) * cols] for i in range(4))]
    reshape x5 -> x0, local copies, waits for them, and re-layouts: 3.48 us -> none  [the longest x3 1.95 us: data_parallel(): join = lambda a: a.reshape(-1)]
    slice x3 -> x0, local copies, waits for them, and re-layouts: 3.2 us -> none  [the longest x1 1.62 us: data_parallel(): sums[V_B2]]
    concatenate x2 -> x0, other arithmetic: 2.33 us -> none  [the longest x1 1.63 us: data_parallel(): packed = jnp.concatenate((w_query, w_key, w_value, w_out), axis=1)]
    unnamed x6 -> x0, local copies, waits for them, and re-layouts: 2.03 us -> none
    pallas_call x1, Pallas kernels: 147 us -> 145 us  [step(): pl.pallas_call(step_kernel, out_shape=(jax.ShapeDtypeStruct((rows, width)...]
where the time goes in v3:
time: 151 us; the launch traced here: 150 us
  Pallas kernels  150 us (99%)
    pallas_call x1, Pallas kernels, step(): pl.pallas_call(step_kernel, out_shape=(jax.ShapeDtypeStruct((rows, width)...  145 us
    pallas_call x1, Pallas kernels, place(): pl.pallas_call(functools.partial(place_kernel, n_t), out_shape=[jax.Shape...  5.01 us

profile of v3, /device:TPU:0, one launch (start us, length us, event | category | flops | bytes accessed | tf_op | source)
XLA Modules:
  0.0 150.4 jit_solution(11050249529041510594)
XLA Ops:
  0.7 144.5 %shard_map.305 = (bf16[512,768]{1,0:T(8,128)(2,1)}, f32[512,768]{1,0:T(8,128)}, f32[3,96,768]{2,1,0:T(8,128)}, f32[16,768]{1,0:T(8,128)}) custom-call(s32[4]{0:T(128)} %length_ref.1, bf16[512,768]{1,0:T(8,128)(2,1)} %x_in.1, bf16[512,768]{1,0:T(8,128)(2,1)} %og_in.1, bf16[96,192]{1,0:T(8,128)(2,1)} %wq.1, bf16[96,192]{1,0:T(8,128)(2,1)} %wk.1, ...), custom_call_target="tpu_custom_call" | custom-call | tf_op jit(solution)/shard_map/pallas_call | solution.py:1082
  145.2 5.0 %shard_map.306 = (bf16[512,768]{1,0:T(8,128)(2,1)}, f32[512,768]{1,0:T(8,128)}, f32[96,192]{1,0:T(8,128)}, f32[96,192]{1,0:T(8,128)}, f32[96,192]{1,0:T(8,128)},...) custom-call(bf16[512,768]{1,0:T(8,128)(2,1)} %get-tuple-element.38.y, ...), custom_call_target="tpu_custom_call" | custom-call | tf_op jit(solution)/shard_map/pallas_call | solution.py:1160

commit v4 on v3

--- a/solution.py
+++ b/solution.py
@@ -484,33 +484,33 @@
             else:
                 self.last(m, q)
 
-    def collect(self, m):
+    def collect(self, m, first=0, stop=4):
+        @pl.loop(0, Z_SIZE)
+        def _(dz):
+            for s in range(first, stop):
+                self.wait(m, 16 + 4 * dz + s)
+
+    def drain(self, m):
+        left = lambda s: self.sem(m, s, s).wait_send()
+        for da in range(1 + self.modes[m]):
+            for slot, _ in self.z_slots(da):
+                left(slot)
+
+            @pl.when(self.mid)
+            def _():
+                left(32 + 2 * da)
+                left(33 + 2 * da)
+
+        for dz in range(1 if self.modes[m] else Z_SIZE):
+            left(4 * dz + 2)
+
+        @pl.loop(0, 8)
+        def _(s):
+            left(2 * s + 1)
+
         @pl.loop(16, 32)
         def _(s):
-            self.wait(m, s)
-
-    def drain(self):
-        for m in range(3):
-            left = lambda s: self.sem(m, s, s).wait_send()
-            for da in range(1 + self.modes[m]):
-                for slot, _ in self.z_slots(da):
-                    left(slot)
-
-                @pl.when(self.mid)
-                def _():
-                    left(32 + 2 * da)
-                    left(33 + 2 * da)
-
-            for dz in range(1 if self.modes[m] else Z_SIZE):
-                left(4 * dz + 2)
-
-            @pl.loop(0, 8)
-            def _(s):
-                left(2 * s + 1)
-
-            @pl.loop(16, 32)
-            def _(s):
-                left(s)
+            left(s)
 
 
 class Scatter(Routes):
@@ -840,15 +840,17 @@
         self.tiles(body)
 
     def outer_back(self, t):
-        self.dact[...] = dot_nn(self.df[...], self.w[2, t])
-
-        def body(r):
-            d = low(self.dact[r, :] * self.slope[t, r, :].astype(jnp.float32))
-            self.slope[t, r, :] = d
-            self.sums[V_BI + t] += fold(d.astype(jnp.float32))
-
-        self.tiles(body)
+        half = self.rows // 2
+        for i in range(2):
+            r = slice(i * half, (i + 1) * half)
+            d = dot_nn(self.df[r, :], self.w[2, t])
+            self.slope[t, r, :] = low(d * self.slope[t, r, :].astype(jnp.float32))
         self.w[2, t] = low(dot_nn(self.df_t[...], self.act[t]))
+        self.sums[V_BI + t] = self.column_sums(self.slope[t])
+
+    def column_sums(self, a):
+        first = lax.broadcasted_iota(jnp.int32, (16, self.rows), 0) == 0
+        return dot_nn(low(first.astype(jnp.float32)), a)[:8]
 
     def inner_back(self, t):
         self.acc[...] += dot_nt(self.slope[t], self.w[1, t])
@@ -886,10 +888,7 @@
             between(j)
 
     def head_sums(self, t):
-        def body(r):
-            self.sums[V_BI + self.n_t + t] += fold(self.qkv[t, r, :].astype(jnp.float32))
-
-        self.tiles(body)
+        self.sums[V_BI + self.n_t + t] = self.column_sums(self.qkv[t])
 
     def project_grad(self, t):
         self.w0_grad[t] = low(dot_nn(self.x_t[...], self.qkv[t]))
@@ -912,36 +911,37 @@
 GATHER_MODES = (0, 1, 1)
 SCATTER_MODES = (0, 1, 1)
 GATHER = {
-    "first": ("A0:0", "y0:0", "B1:0"),
-    "start": ("B0:0", "A2:0", "A1:0", "y1:0", "p0:4", "p0:1", "l0:0", "p0:2", "p1:2", "y2:0", "l0:1", "p0:5", "l0:4", "p0:3",
-        "p0:6-7", "p1:1", "l0:5", "l1:2", "p2:2", "l0:6", "p2:1", "p1:5", "l0:3", "l0:2", "l0:7", "p1:3"),
+    "first": ("y0:0", "A0:0", "A1:0", "p0:4", "B1:0", "y2:0", "B0:0", "l0:4", "p0:1"),
+    "start": ("p0:2", "p1:1", "y1:0", "l0:0", "p0:3", "p0:6", "p0:5", "l0:2", "l0:1", "l1:1", "p0:7", "p2:2", "p1:2", "p1:5",
+        "l0:5", "B2:0", "l0:6", "A2:0", "l0:3", "l0:7"),
     "attend": (),
-    "heads": {3: ("l1:0",), 4: ("l1:5", "l1:1"), 5: ("l2:2", "p1:6"), 6: ("p1:4", "p2:5"), 8: ("l1:6", "l1:3"), 9: ("p2:3",),
-        10: ("l1:4", "l2:0"), 11: ("p2:6",)},
-    "out": {1: ("B2:0",), 2: ("l2:1", "p1:7"), 3: ("l1:7",)},
-    "norm": ("p2:4",),
-    "ffn": ("l2:6",),
-    "inner": {0: ("p2:7",), 2: ("l2:4", "l2:3", "l2:5", "l2:7")},
+    "heads": {4: ("l2:0", "p2:3", "p2:1"), 8: ("p1:4", "p1:7", "l1:0", "l1:5"), 10: ("l2:3",), 11: ("l1:4", "l2:2", "l1:6",
+        "p2:4", "l1:3", "l1:2")},
+    "out": {0: ("p1:6", "p1:3"), 3: ("p2:5", "l1:7")},
+    "norm": (),
+    "ffn": ("p2:6",),
+    "inner": {1: ("p2:7", "l2:6", "l2:1", "l2:5", "l2:4"), 3: ("l2:7",)},
+    "outer": {},
+    "late": (),
 }
 SCATTER = {
-    "outer": {},
-    "inner": {0: ("b2:0",), 1: ("b2:2",), 2: ("b2:1", "z2:0", "b2:4", "b2:3")},
-    "norm": ("b2:5",),
-    "heads": {0: ("b1:2",), 2: ("z2:2", "b1:0"), 5: ("z2:3", "b2:6", "b1:1"), 7: ("b1:3", "b1:6"), 8: ("z1:1",), 9:
-        ("e2:0",), 10: ("z1:0",)},
-    "grad": {0: ("b1:4",), 1: ("z2:1",), 3: ("b0:0", "b1:7", "z1:2", "b0:2", "b1:5", "b0:4", "b0:1")},
-    "last": ((), (), ("e1:0", "z1:3", "b0:6", "b0:3", "a0:0", "b0:5", "a0:1", "z0:0", "a0:2", "z0:1", "b0:7"), ("b2:7",
-        "F2:0", "a0:3", "F1:0", "F0:0")),
+    "outer": {3: ("b2:0",)},
+    "inner": {0: ("b2:2",), 1: ("z2:0",), 2: ("b2:3", "b2:1", "b2:5")},
+    "norm": ("b2:4", "b1:2", "b2:7"),
+    "heads": {2: ("z2:1",), 4: ("z2:2-3",), 7: ("z1:1", "b1:6"), 8: ("b1:1", "z1:0")},
+    "grad": {0: ("b1:0", "b1:4"), 1: ("b1:3",), 3: ("b1:5", "z1:2", "b0:0")},
+    "last": (("z1:3", "b0:2"), ("b0:4", "b0:1"), ("a0:0", "b1:7", "b2:6", "e2:0", "e1:0", "b0:3", "b0:6", "a0:1", "b0:5",
+        "z0:0", "b0:7"), ("a0:2", "z0:1", "F1:0", "F2:0", "a0:3", "F0:0")),
 }
 
 
 def step_kernel(
     length_ref, x_in, og_in, wq, wk, wv, wo, w_inner, w_outer, b_outer, b_value, b_out, gain1, bias1, gain2, bias2, b_query, b_inner,
-    y_ref, acc_ref, out_ref, vout_ref,
+    y_out, acc_out, shards_out, vout_ref,
     x_ref, og_ref, parts, vec_ref, qkv_bias, inner_bias,
-    w, sums, qkv, p, att, z1, inv1, h1b, ffn, df, datt, dact, x_t, h1b_t, df_t,
+    w, sums, qkv, p, att, z1, inv1, h1b, ffn, df, datt, x_t, h1b_t, df_t, y_ref, acc_ref, out_ref,
     core_buf, b_buf, t_buf, vec_buf, vec_z,
-    load_sem, gather_send, gather_recv, send_sem, recv_sem, vec_send, vec_recv,
+    load_sem, store_sem, gather_send, gather_recv, send_sem, recv_sem, vec_send, vec_recv,
 ):
     me = Place()
     rows, width = x_ref.shape
@@ -951,7 +951,7 @@
     small = VectorSum(me, vec_buf, vec_z, vec_send, vec_recv)
     a = Layer(
         x=x_ref, og=og_ref, w=w, w0_grad=w0_grad, qkv_bias=qkv_bias, inner_bias=inner_bias, vec=vec_ref, y=y_ref, acc=acc_ref, sums=sums,
-        qkv=qkv, p=p, att=att, z1=z1, inv1=inv1, h1b=h1b, act=act, slope=slope, df=df, datt=datt, dact=dact, x_t=x_t, h1b_t=h1b_t, df_t=df_t,
+        qkv=qkv, p=p, att=att, z1=z1, inv1=inv1, h1b=h1b, act=act, slope=slope, df=df, datt=datt, x_t=x_t, h1b_t=h1b_t, df_t=df_t,
     )
     vectors = (b_outer, b_value, b_out, gain1, bias1, gain2, bias2, b_query)
     pairs = [(ref, parts.at[i]) for i, ref in enumerate((wq, wk, wv, wo))]
@@ -1012,15 +1012,26 @@
         a.inner(t)
         at(gather.run, GATHER["inner"], t)
 
-    gather.collect(2)
-
-    @pl.loop(0, a.n_t)
-    def _(t):
-        a.outer(t)
+    gather.collect(2, 0, 3)
+    gather.run(GATHER["late"])
+
+    @pl.loop(0, 2)
+    def _(core):
+        a.outer(2 * me.y + core)
+        at(gather.run, GATHER["outer"], core)
+
+    gather.collect(2, 3, 4)
+
+    @pl.loop(0, 2)
+    def _(core):
+        a.outer(2 * (1 - me.y) + core)
 
     a.second_norm(length)
     a.transpose(a.df, a.df_t)
-    gather.drain()
+    stores = [(y_ref, y_out), (acc_ref, acc_out), (out_ref, shards_out)]
+    stores = [pltpu.make_async_copy(src, dst, store_sem.at[i]) for i, (src, dst) in enumerate(stores)]
+    stores[0].start()
+    gather.drain(2)
 
     @pl.loop(0, a.n_t)
     def _(i):
@@ -1028,6 +1039,8 @@
         scatter.ready(2, i)
         at(scatter.run, SCATTER["outer"], i)
 
+    gather.drain(1)
+
     @pl.loop(0, a.n_t)
     def _(i):
         a.inner_back(scatter.order(i))
@@ -1062,8 +1075,13 @@
         if t in (1, 3):
             small.advance((t + 1) // 2)
         scatter.run(steps)
+    stores[1].start()
     vout_ref[...] = small.result()
+    stores[2].start()
+    gather.drain(0)
     scatter.drain()
+    for store in stores:
+        store.wait()
 
 
 def step(seq_lengths, x, og, weights, vectors, b_inner, n_t):
@@ -1088,7 +1106,7 @@
             jax.ShapeDtypeStruct((n_v, width), f32),
         ),
         in_specs=[pl.BlockSpec(memory_space=pltpu.SMEM)] + [anywhere] * n_loads,
-        out_specs=[vmem] * 4,
+        out_specs=[anywhere] * 3 + [vmem],
         scratch_shapes=[
             pltpu.VMEM((rows, width), bf),
             pltpu.VMEM((rows, width), bf),
@@ -1107,16 +1125,19 @@
             pltpu.VMEM((n_t, max(2 * rows, width), width), bf),
             pltpu.VMEM((rows, width), bf),
             pltpu.VMEM((rows, owidth), bf),
-            pltpu.VMEM((rows, width), f32),
             pltpu.VMEM((width, rows), bf),
             pltpu.VMEM((width, rows), bf),
             pltpu.VMEM((width, rows), bf),
+            pltpu.VMEM((rows, width), bf),
+            pltpu.VMEM((rows, width), f32),
+            pltpu.VMEM((3, shard, width), f32),
             buf(16),
             buf(8),
             buf(9),
             pltpu.VMEM((7, n_v, width), f32),
             pltpu.VMEM((Z_SIZE, n_v, width), f32),
             dma((n_loads,)),
+            dma((3,)),
             dma((3, 36)),
             dma((3, 36)),
             dma((3, 33)),
@@ -1128,34 +1149,48 @@
     )(seq_lengths, x, og, *weights, *vectors, b_inner)
 
 
-def place_kernel(n_t, y_in, gin_in, shards, sums, y, gin, gq, gk, gv, go, gi, gf, bq, bv, bo, g1, b1, bi, bf, g2, b2, y_buf, gin_buf, sems):
-    first = [pltpu.make_async_copy(y_in, y_buf, sems.at[0]), pltpu.make_async_copy(gin_in, gin_buf, sems.at[1])]
-    then = [pltpu.make_async_copy(y_buf, y, sems.at[2]), pltpu.make_async_copy(gin_buf, gin, sems.at[3])]
-    direct = [pltpu.make_async_copy(shards.at[i], ref, sems.at[3 + i]) for i, ref in ((1, gi), (2, gf))]
-    for copy in first + direct:
-        copy.start()
+def place_kernel(n_t, y_in, gin_in, shards_in, sums_in, *refs):
+    y, gin, gq, gk, gv, go, gi, gf, bq, bv, bo, g1, b1, bi, bf, g2, b2, y_buf, gin_buf, shards, sums, parts, heads, sems = refs
     cols = gq.shape[1]
+    started = []
+
+    def copy(src, dst):
+        started.append(pltpu.make_async_copy(src, dst, sems.at[len(started)]))
+        started[-1].start()
+        return started[-1]
+
+    pairs = [(sums_in, sums), (shards_in, shards), (gin_in, gin_buf), (y_in, y_buf)]
+    loads = [copy(src, dst) for src, dst in pairs]
+    loads[0].wait()
+    for row, ref in ((V_BO, bo), (V_G1, g1), (V_B1, b1), (V_BF, bf), (V_G2, g2), (V_B2, b2)):
+        copy(sums.at[row], ref)
+    for t in range(n_t):
+        copy(sums.at[V_BI + t], bi.at[t, 0])
+        row = sums[V_BI + n_t + t : V_BI + n_t + t + 1, :]
+        heads[0:1, t * cols : (t + 1) * cols] = row[:, :cols]
+        heads[1:2, t * cols : (t + 1) * cols] = row[:, 2 * cols : 3 * cols]
+    loads[1].wait()
+    copy(shards.at[1], gi)
+    copy(shards.at[2], gf)
+    for i in range(4):
+        parts[i] = shards[0, :, i * cols : (i + 1) * cols]
+    copy(heads.at[0], bq)
+    copy(heads.at[1], bv)
+    loads[2].wait()
+    copy(gin_buf, gin)
     for i, ref in enumerate((gq, gk, gv, go)):
-        ref[...] = shards[0, :, i * cols : (i + 1) * cols]
-    for row, ref in ((V_BO, bo), (V_G1, g1), (V_B1, b1), (V_BF, bf), (V_G2, g2), (V_B2, b2)):
-        ref[...] = sums[row : row + 1, :].reshape(ref.shape)
-    for t in range(n_t):
-        bi[t] = sums[V_BI + t : V_BI + t + 1, :]
-    heads = [sums[V_BI + n_t + t : V_BI + n_t + t + 1, :] for t in range(n_t)]
-    bq[...] = jnp.concatenate([h[:, :cols] for h in heads], axis=1).reshape(bq.shape)
-    bv[...] = jnp.concatenate([h[:, 2 * cols : 3 * cols] for h in heads], axis=1).reshape(bv.shape)
-    for copy, after in zip(first, then):
-        copy.wait()
-        after.start()
-    for copy in direct + then:
-        copy.wait()
+        copy(parts.at[i], ref)
+    loads[3].wait()
+    copy(y_buf, y)
+    for done in started[len(loads) :]:
+        done.wait()
 
 
 def place(y, gin, shards, sums, n_t):
     shard, width = shards.shape[1:]
     cols = width // n_t
     f32 = jnp.float32
-    vmem, anywhere = pl.BlockSpec(memory_space=pltpu.VMEM), pl.BlockSpec(memory_space=pl.ANY)
+    anywhere = pl.BlockSpec(memory_space=pl.ANY)
     row = jax.ShapeDtypeStruct((width,), f32)
     return pl.pallas_call(
         functools.partial(place_kernel, n_t),
@@ -1167,9 +1202,17 @@
             + [jax.ShapeDtypeStruct((n_t, 1, width), f32)]
             + [row] * 3
         ),
-        in_specs=[anywhere, anywhere, vmem, vmem],
-        out_specs=[anywhere] * 2 + [vmem] * 4 + [anywhere] * 2 + [vmem] * 9,
-        scratch_shapes=[pltpu.VMEM(y.shape, y.dtype), pltpu.VMEM(gin.shape, f32), pltpu.SemaphoreType.DMA((6,))],
+        in_specs=[anywhere] * 4,
+        out_specs=[anywhere] * 17,
+        scratch_shapes=[
+            pltpu.VMEM(y.shape, y.dtype),
+            pltpu.VMEM(gin.shape, f32),
+            pltpu.VMEM(shards.shape, f32),
+            pltpu.VMEM(sums.shape, f32),
+            pltpu.VMEM((4, shard, cols), f32),
+            pltpu.VMEM((8, width), f32),
+            pltpu.SemaphoreType.DMA((20 + n_t,)),
+        ],
     )(y, gin, shards, sums)
 
 

time: 151 us -> 144 us (0.954)
  Pallas kernels: 150 us -> 143 us
    pallas_call x1, Pallas kernels: 145 us -> 140 us  [step(): pl.pallas_call(step_kernel, out_shape=(jax.ShapeDtypeStruct((rows, width)...]
    pallas_call x1, Pallas kernels: 5.01 us -> 3.45 us  [place(): pl.pallas_call(functools.partial(place_kernel, n_t), out_shape=[jax.Shape...]
where the time goes in v4:
time: 144 us
  Pallas kernels  143 us (99%)
    pallas_call x1, Pallas kernels, step(): pl.pallas_call(step_kernel, out_shape=(jax.ShapeDtypeStruct((rows, width)...  140 us
    pallas_call x1, Pallas kernels, place(): pl.pallas_call(functools.partial(place_kernel, n_t), out_shape=[jax.Shape...  3.45 us

profile of v4, /device:TPU:0, one launch (start us, length us, event | category | flops | bytes accessed | tf_op | source)
XLA Modules:
  0.0 144.2 jit_solution(6608651866682751087)
XLA Ops:
  0.7 139.9 %shard_map.305 = (bf16[512,768]{1,0:T(8,128)(2,1)}, f32[512,768]{1,0:T(8,128)}, f32[3,96,768]{2,1,0:T(8,128)}, f32[16,768]{1,0:T(8,128)}) custom-call(s32[4]{0:T(128)} %length_ref.1, bf16[512,768]{1,0:T(8,128)(2,1)} %x_in.1, bf16[512,768]{1,0:T(8,128)(2,1)} %og_in.1, bf16[96,192]{1,0:T(8,128)(2,1)} %wq.1, bf16[96,192]{1,0:T(8,128)(2,1)} %wk.1, ...), custom_call_target="tpu_custom_call" | custom-call | tf_op jit(solution)/shard_map/pallas_call | solution.py:1100
  140.6 3.5 %shard_map.306 = (bf16[512,768]{1,0:T(8,128)(2,1)}, f32[512,768]{1,0:T(8,128)}, f32[96,192]{1,0:T(8,128)}, f32[96,192]{1,0:T(8,128)}, f32[96,192]{1,0:T(8,128)},...) custom-call(bf16[512,768]{1,0:T(8,128)(2,1)} %get-tuple-element.38.y, ...), custom_call_target="tpu_custom_call" | custom-call | tf_op jit(solution)/shard_map/pallas_call | solution.py:1195

commit v5 on v4

--- a/solution.py
+++ b/solution.py
@@ -1072,8 +1072,12 @@
 
     for t, steps in enumerate(SCATTER["last"]):
         a.project_back(t)
-        if t in (1, 3):
-            small.advance((t + 1) // 2)
+        if t == 1:
+            small.advance(1)
+        if t == 2:
+            scatter.run(steps[:3])
+            small.advance(2)
+            steps = steps[3:]
         scatter.run(steps)
     stores[1].start()
     vout_ref[...] = small.result()

time: 144 us -> 143 us (level)
  Pallas kernels: 143 us -> 141 us
    pallas_call x1, Pallas kernels: 140 us -> 138 us  [step(): pl.pallas_call(step_kernel, out_shape=(jax.ShapeDtypeStruct((rows, width)...]
where the time goes in v5:
time: 143 us; the launch traced here: 142 us
  Pallas kernels  141 us (99%)
    pallas_call x1, Pallas kernels, step(): pl.pallas_call(step_kernel, out_shape=(jax.ShapeDtypeStruct((rows, width)...  138 us
    pallas_call x1, Pallas kernels, place(): pl.pallas_call(functools.partial(place_kernel, n_t), out_shape=[jax.Shape...  3.45 us

profile of v5, /device:TPU:0, one launch (start us, length us, event | category | flops | bytes accessed | tf_op | source)
XLA Modules:
  0.0 141.9 jit_solution(828698296299488981)
XLA Ops:
  0.7 137.6 %shard_map.305 = (bf16[512,768]{1,0:T(8,128)(2,1)}, f32[512,768]{1,0:T(8,128)}, f32[3,96,768]{2,1,0:T(8,128)}, f32[16,768]{1,0:T(8,128)}) custom-call(s32[4]{0:T(128)} %length_ref.1, bf16[512,768]{1,0:T(8,128)(2,1)} %x_in.1, bf16[512,768]{1,0:T(8,128)(2,1)} %og_in.1, bf16[96,192]{1,0:T(8,128)(2,1)} %wq.1, bf16[96,192]{1,0:T(8,128)(2,1)} %wk.1, ...), custom_call_target="tpu_custom_call" | custom-call | tf_op jit(solution)/shard_map/pallas_call | solution.py:1104
  138.3 3.5 %shard_map.306 = (bf16[512,768]{1,0:T(8,128)(2,1)}, f32[512,768]{1,0:T(8,128)}, f32[96,192]{1,0:T(8,128)}, f32[96,192]{1,0:T(8,128)}, f32[96,192]{1,0:T(8,128)},...) custom-call(bf16[512,768]{1,0:T(8,128)(2,1)} %get-tuple-element.38.y, ...), custom_call_target="tpu_custom_call" | custom-call | tf_op jit(solution)/shard_map/pallas_call | solution.py:1199

commit v6 on v5

--- a/solution.py
+++ b/solution.py
@@ -1028,7 +1028,7 @@
 
     a.second_norm(length)
     a.transpose(a.df, a.df_t)
-    stores = [(y_ref, y_out), (acc_ref, acc_out), (out_ref, shards_out)]
+    stores = [(y_ref, y_out), (acc_ref, acc_out)] + [(out_ref.at[m], shards_out.at[m]) for m in range(3)]
     stores = [pltpu.make_async_copy(src, dst, store_sem.at[i]) for i, (src, dst) in enumerate(stores)]
     stores[0].start()
     gather.drain(2)
@@ -1078,8 +1078,12 @@
             scatter.run(steps[:3])
             small.advance(2)
             steps = steps[3:]
+        if t == a.n_t - 1:
+            scatter.run(steps[:-1])
+            for store in (stores[1], stores[3], stores[4]):
+                store.start()
+            steps = steps[-1:]
         scatter.run(steps)
-    stores[1].start()
     vout_ref[...] = small.result()
     stores[2].start()
     gather.drain(0)
@@ -1141,7 +1145,7 @@
             pltpu.VMEM((7, n_v, width), f32),
             pltpu.VMEM((Z_SIZE, n_v, width), f32),
             dma((n_loads,)),
-            dma((3,)),
+            dma((5,)),
             dma((3, 36)),
             dma((3, 36)),
             dma((3, 33)),

time: 143 us -> 142 us (level)
  no operation moved by 1% of the time
where the time goes in v6:
time: 142 us; the launch traced here: 141 us
  Pallas kernels  140 us (99%)
    pallas_call x1, Pallas kernels, step(): pl.pallas_call(step_kernel, out_shape=(jax.ShapeDtypeStruct((rows, width)...  137 us
    pallas_call x1, Pallas kernels, place(): pl.pallas_call(functools.partial(place_kernel, n_t), out_shape=[jax.Shape...  3.45 us

profile of v6, /device:TPU:0, one launch (start us, length us, event | category | flops | bytes accessed | tf_op | source)
XLA Modules:
  0.0 141.3 jit_solution(6685683808256222104)
XLA Ops:
  0.7 137.0 %shard_map.305 = (bf16[512,768]{1,0:T(8,128)(2,1)}, f32[512,768]{1,0:T(8,128)}, f32[3,96,768]{2,1,0:T(8,128)}, f32[16,768]{1,0:T(8,128)}) custom-call(s32[4]{0:T(128)} %length_ref.1, bf16[512,768]{1,0:T(8,128)(2,1)} %x_in.1, bf16[512,768]{1,0:T(8,128)(2,1)} %og_in.1, bf16[96,192]{1,0:T(8,128)(2,1)} %wq.1, bf16[96,192]{1,0:T(8,128)(2,1)} %wk.1, ...), custom_call_target="tpu_custom_call" | custom-call | tf_op jit(solution)/shard_map/pallas_call | solution.py:1108
  137.7 3.5 %shard_map.306 = (bf16[512,768]{1,0:T(8,128)(2,1)}, f32[512,768]{1,0:T(8,128)}, f32[96,192]{1,0:T(8,128)}, f32[96,192]{1,0:T(8,128)}, f32[96,192]{1,0:T(8,128)},...) custom-call(bf16[512,768]{1,0:T(8,128)(2,1)} %get-tuple-element.38.y, ...), custom_call_target="tpu_custom_call" | custom-call | tf_op jit(solution)/shard_map/pallas_call | solution.py:1203
